TPU v7x, 32 devices: a whole 2x2x4 slice. The times are simulated.
32 devices in a mesh: gx: 4 (over y, x), gy: 8 (over z, core).
Axes of the slice: x: 2, y: 2, z: 4, core: 2. Of those that a mesh axis runs over, the one named last changes fastest.
Arguments:
- inputs: bfloat16 [32, 32, 32, 256], P(None, 'gx', 'gy'), may hold values from -6 to 6
- pre_act: bfloat16 [32, 32, 32, 256], P(None, 'gx', 'gy'), may hold values from -8 to 8
- grad_out: bfloat16 [32, 32, 32, 256], P(None, 'gx', 'gy'), may hold values from -6 to 6
- point_weight: float32 [32, 32], replicated, may hold values from -1 to 1
- mode_weight: float32 [32, 32, 2, 16, 1024], P('gx', 'gy'), may hold values from -12 to 12
Outputs:
- input_grad: float32 [32, 32, 32, 256], P(None, 'gx', 'gy')
- point_grad: float32 [32, 32], replicated
- bias_grad: float32 [32], replicated
- mode_grad: float32 [32, 32, 2, 16, 1024], P('gx', 'gy')
All inputs are finite; a program needn't handle non-finite values.
Results may differ from a plain program's by a relative error of at most 0.0003.
Values sent between devices are 32-bit elements; how exact they have to be, the bound alone decides.
No kernel may reach another device: no remote copies, remote signals or barrier semaphores. Data moves between devices by JAX's collectives and lax.ppermute only.
A program may use at most 64 MiB of HBM per device.

v0:
```python
import math

import jax
import jax.numpy as jnp
import numpy as np
from jax import lax
from jax.experimental import pallas as pl
from jax.experimental.pallas import tpu as pltpu
from jax.sharding import PartitionSpec as P

HIGHEST_PRECISION = lax.Precision.HIGHEST
ROOT_HALF = 0.7071067811865476
NORMAL_PEAK = 0.3989422804014327


def gelu_slope(pre_act):
    value = pre_act.astype(jnp.float32)
    return (
        0.5 * (1.0 + jax.scipy.special.erf(value * ROOT_HALF))
        + value * jnp.exp(-0.5 * value * value) * NORMAL_PEAK
    )


def phases(length, modes, wrapped, index, first, count):
    if wrapped:
        frequency = jnp.where(index < modes // 2, index, index + (length - modes))
    else:
        frequency = index
    places = first + jnp.arange(count, dtype=jnp.int32)
    turns = frequency[:, None] * places[None, :] % length
    angle = turns.astype(jnp.float32) * (2.0 * math.pi / length)
    return (jnp.cos(angle), jnp.sin(angle))


def transform(cos_table, sin_table, data, sign):
    real_part = data[..., 0, :]
    imag_part = data[..., 1, :]

    def apply(table, values):
        return jnp.tensordot(table, values, axes=1, precision=HIGHEST_PRECISION)

    if sign < 0:
        out_real = apply(cos_table, real_part) + apply(sin_table, imag_part)
        out_imag = apply(cos_table, imag_part) - apply(sin_table, real_part)
    else:
        out_real = apply(cos_table, real_part) - apply(sin_table, imag_part)
        out_imag = apply(cos_table, imag_part) + apply(sin_table, real_part)
    return jnp.stack([out_real, out_imag], axis=-2)


def depth_forward(field, kz_count):
    channels = field.shape[0]
    depth = field.shape[-1]
    cos_z, sin_z = phases(depth, kz_count, False, jnp.arange(kz_count, dtype=jnp.int32), 0, depth)
    real_part = jnp.einsum("cabz,kz->abkc", field, cos_z, precision=HIGHEST_PRECISION)
    imag_part = -jnp.einsum("cabz,kz->abkc", field, sin_z, precision=HIGHEST_PRECISION)
    lead = real_part.shape[:2]
    return jnp.stack(
        [
            real_part.reshape(lead + (kz_count * channels,)),
            imag_part.reshape(lead + (kz_count * channels,)),
        ],
        axis=2,
    )


def depth_inverse(spectrum, kz_count, channels, depth):
    lead = spectrum.shape[:2]
    split = spectrum.reshape(lead + (2, kz_count, channels))
    cos_z, sin_z = phases(depth, kz_count, False, jnp.arange(kz_count, dtype=jnp.int32), 0, depth)
    return jnp.einsum(
        "abkc,kz->cabz", split[:, :, 0], cos_z, precision=HIGHEST_PRECISION
    ) - jnp.einsum("abkc,kz->cabz", split[:, :, 1], sin_z, precision=HIGHEST_PRECISION)


def mode_work(spectrum_in, spectrum_grad, weight, cells):
    rows_a, rows_b, _, kz_count, _ = weight.shape
    channels = spectrum_in.shape[-1] // kz_count
    factor = (
        jnp.where(jnp.arange(kz_count, dtype=jnp.int32) == 0, 1.0, 2.0).astype(jnp.float32) / cells
    )
    shape = (rows_a, rows_b, 2, kz_count, channels)
    given = spectrum_in.reshape(shape)
    scaled = spectrum_grad.reshape(shape) * factor[:, None]
    mixing = weight.reshape(shape + (channels,))
    in_real = given[:, :, 0]
    in_imag = given[:, :, 1]
    grad_real = scaled[:, :, 0]
    grad_imag = scaled[:, :, 1]
    mix_real = mixing[:, :, 0]
    mix_imag = mixing[:, :, 1]

    def outer(left, right):
        return jnp.einsum("abki,abko->abkio", left, right, precision=HIGHEST_PRECISION)

    def mixed(values, matrix):
        return jnp.einsum("abko,abkio->abki", values, matrix, precision=HIGHEST_PRECISION)

    result_real = outer(in_real, grad_real) + outer(in_imag, grad_imag)
    result_imag = outer(in_real, grad_imag) - outer(in_imag, grad_real)
    mode_grad = jnp.stack([result_real, result_imag], axis=2).reshape(
        rows_a, rows_b, 2, kz_count, channels * channels
    )
    back_real = mixed(grad_real, mix_real) + mixed(grad_imag, mix_imag)
    back_imag = mixed(grad_imag, mix_real) - mixed(grad_real, mix_imag)
    back_spectrum = jnp.stack([back_real, back_imag], axis=2).reshape(
        rows_a, rows_b, 2, kz_count * channels
    )
    return (mode_grad, back_spectrum)


def joined_rows(main, extra):
    count = main.shape[0]
    return jnp.concatenate([main.reshape(count, -1), extra.reshape(count, -1)], axis=1)


def split_rows(result, main_shape, extra_shape):
    main_size = 1
    for item in main_shape[1:]:
        main_size = main_size * item
    main = result[:, :main_size].reshape(main_shape)
    extra = result[:, main_size:].reshape(extra_shape)
    return (main, extra)


def partial_sums(inputs, pre_act, grad_out, point_weight, mode_weight):
    channels, x_local, y_local, depth = inputs.shape
    kx_local, ky_local, _, kz_count, _ = mode_weight.shape
    x_devices = lax.axis_size("gx")
    y_devices = lax.axis_size("gy")
    x_length = x_local * x_devices
    y_length = y_local * y_devices
    kx_count = kx_local * x_devices
    ky_count = ky_local * y_devices
    cells = x_length * y_length * depth
    scale = 1.0 / math.sqrt(cells)
    x_offset = lax.axis_index("gx") * x_local
    y_offset = lax.axis_index("gy") * y_local
    width = kz_count * channels
    pair_width = 2 * width
    stat_count = channels * channels + channels
    mode_count = kx_count * ky_count
    field_in = inputs.astype(jnp.float32)
    pre_grad = grad_out.astype(jnp.float32) * gelu_slope(pre_act)
    weight_sum = jnp.einsum("ixyz,oxyz->io", field_in, pre_grad, precision=HIGHEST_PRECISION)
    bias_sum = jnp.sum(pre_grad, axis=(1, 2, 3))
    extra_cols = (stat_count + mode_count - 1) // mode_count
    stat_flat = jnp.concatenate([weight_sum.reshape(-1), bias_sum])
    grid = jnp.pad(stat_flat, (0, mode_count * extra_cols - stat_count)).reshape(
        kx_count, ky_count, extra_cols
    )
    spectra = jnp.stack(
        [depth_forward(field_in, kz_count), depth_forward(pre_grad, kz_count)], axis=2
    )
    along_y = jnp.swapaxes(spectra, 0, 1)
    grid_y = jnp.swapaxes(grid, 0, 1)
    cos_y, sin_y = phases(
        y_length,
        ky_count,
        True,
        jnp.arange(lax.axis_size("gy") * ky_local, dtype=jnp.int32),
        y_offset,
        y_local,
    )
    partial_y, extra_y = split_rows(
        lax.psum_scatter(
            joined_rows(transform(cos_y, sin_y, along_y, -1), grid_y),
            "gy",
            scatter_dimension=0,
            tiled=True,
        ),
        (ky_local, x_local, 2, 2, width),
        (ky_local, kx_count, extra_cols),
    )
    along_x = jnp.swapaxes(partial_y, 0, 1)
    extra_along = jnp.swapaxes(extra_y, 0, 1)
    cos_x, sin_x = phases(
        x_length,
        kx_count,
        True,
        jnp.arange(lax.axis_size("gx") * kx_local, dtype=jnp.int32),
        x_offset,
        x_local,
    )
    owned, owned_extra = split_rows(
        lax.psum_scatter(
            joined_rows(transform(cos_x, sin_x, along_x, -1), extra_along),
            "gx",
            scatter_dimension=0,
            tiled=True,
        ),
        (kx_local, ky_local, 2, 2, width),
        (kx_local, ky_local, extra_cols),
    )
    mode_grad, back_spectrum = mode_work(owned[:, :, 0], owned[:, :, 1], mode_weight, cells)
    back_joined = jnp.concatenate(
        [back_spectrum.reshape(kx_local, ky_local, pair_width), owned_extra], axis=2
    )
    piece = lax.all_gather(back_joined, "gx", axis=0, tiled=True)
    kx_index = jnp.arange(piece.shape[0], dtype=jnp.int32)
    cos_x, sin_x = phases(x_length, kx_count, True, kx_index, x_offset, x_local)
    main = piece[:, :, :pair_width].reshape(piece.shape[0], piece.shape[1], 2, width)
    near = transform(cos_x.T, sin_x.T, main, 1)
    near_stats = piece[:, :, pair_width:]
    side_cols = (kx_count * extra_cols + x_local - 1) // x_local
    side_flat = jnp.swapaxes(near_stats, 0, 1).reshape(ky_local, kx_count * extra_cols)
    side = jnp.swapaxes(side_flat.reshape(ky_local, x_local, side_cols), 0, 1)
    near_joined = jnp.concatenate([near.reshape(x_local, ky_local, pair_width), side], axis=2)
    piece = lax.all_gather(near_joined, "gy", axis=1, tiled=True)
    ky_index = jnp.arange(piece.shape[1], dtype=jnp.int32)
    cos_y, sin_y = phases(y_length, ky_count, True, ky_index, y_offset, y_local)
    main = piece[:, :, :pair_width].reshape(piece.shape[0], piece.shape[1], 2, width)
    moved = jnp.swapaxes(transform(cos_y.T, sin_y.T, jnp.swapaxes(main, 0, 1), 1), 0, 1)
    far_stats = piece[:, :, pair_width:]
    stats_rows = jnp.swapaxes(far_stats, 0, 1).reshape(ky_count, x_local * side_cols)
    stats_grid = jnp.swapaxes(stats_rows.reshape(ky_count, kx_count, extra_cols), 0, 1)
    stat_values = stats_grid.reshape(-1)[:stat_count]
    point_grad = stat_values[: channels * channels].reshape(channels, channels)
    bias_grad = stat_values[channels * channels :]
    local = jnp.einsum("io,oxyz->ixyz", point_weight, pre_grad, precision=HIGHEST_PRECISION)
    input_grad = local + depth_inverse(moved, kz_count, channels, depth)
    return (input_grad, point_grad * scale, bias_grad * scale, mode_grad)


LANES = 128
SUBLANES = 8
HL = 8
BF16 = jnp.bfloat16
F32 = jnp.float32


def split_table(table):
    high = table.astype(np.float32).astype(BF16)
    low = (table - high.astype(np.float64)).astype(np.float32).astype(BF16)
    return (high, low)


def split(values):
    high = values.astype(BF16)
    return (high, (values - high.astype(F32)).astype(BF16))


def dot(left, right):
    return jnp.dot(left, right, preferred_element_type=F32)


def dot_rows(left, right):
    return lax.dot_general(left, right, (((1,), (1,)), ((), ())), preferred_element_type=F32)


def product(left, right, multiply=dot):
    return (
        multiply(left[0], right[0]) + multiply(left[0], right[1]) + multiply(left[1], right[0])
    )


def iota(shape, axis):
    return lax.broadcasted_iota(jnp.int32, shape, axis)


def wave(length, modes):
    index = np.arange(modes)
    frequency = np.where(index < modes // 2, index, index + (length - modes))
    turns = frequency[:, None] * np.arange(length)[None, :] % length
    angle = turns * (2.0 * math.pi / length)
    return (np.cos(angle), np.sin(angle))


def depth_table(depth, kz_count, x_local):
    h = np.arange(kz_count)
    angle = (h[None, :] * np.arange(LANES)[:, None] % depth) * (2.0 * math.pi / depth)
    both = np.stack([np.cos(angle), -np.sin(angle)], axis=1)
    both = both.reshape(LANES, 2, kz_count // HL, 1, HL).transpose(0, 2, 3, 1, 4)
    return np.broadcast_to(both, (LANES, kz_count // HL, x_local, 2, HL)).reshape(LANES, -1)


def x_table(x_devices, x_local, kx_local):
    cos_x, sin_x = wave(x_devices * x_local, x_devices * kx_local)
    mix = np.array([[cos_x, -sin_x], [sin_x, cos_x]])
    mix = mix.reshape(2, 2, x_devices, kx_local, x_devices, x_local)
    full = np.einsum("pqakbx,hj->bxphaqkj", mix, np.eye(HL))
    size = x_devices * x_local * 2 * HL
    return full.reshape(size, -1)


def y_table(y_devices, y_local, ky_local, hh_count):
    pair = wave(y_devices * y_local, y_devices * ky_local)
    shape = (y_devices, ky_local, y_devices, y_local)
    parts = [
        np.einsum("akby,fg,hi->akgibfhy", t.reshape(shape), np.eye(2), np.eye(hh_count)).reshape(
            y_devices * ky_local * 2 * hh_count, -1
        )
        for t in pair
    ]
    return np.concatenate(parts, axis=1)


def y_inverse_table(y_devices, y_local, ky_local, hh_count):
    pair = wave(y_devices * y_local, y_devices * ky_local)
    shape = (y_devices, ky_local, y_devices, y_local)
    parts = [
        np.einsum("akby,hi->biyakh", t.reshape(shape), np.eye(hh_count)).reshape(
            y_devices * y_local * hh_count, -1
        )
        for t in pair
    ]
    return np.concatenate(parts, axis=1)


def spread_table(channels):
    left = np.repeat(np.eye(channels), channels, axis=1)
    right = np.tile(np.eye(channels), (1, LANES // channels))
    one = np.zeros((2 * channels, channels * channels + LANES))
    one[:channels, : channels * channels] = left
    one[channels:, channels * channels :] = right
    return np.concatenate([one, one], axis=0).astype(BF16)


def slot_mask(y_local):
    shape = (SUBLANES, LANES)
    return (iota(shape, 0) < y_local) & (iota(shape, 1) % (2 * HL) == HL)


def grid_kernel(in_ref, pre_ref, out_grad_ref, hi_ref, lo_ref, s_ref, ghi_ref, glo_ref):
    channels, x_local = in_ref.shape[:2]
    y_local = SUBLANES // 2
    rows = channels * SUBLANES
    table_hi = hi_ref[...].astype(F32)
    table_lo = lo_ref[...].astype(F32)
    lane_x = iota(table_hi.shape, 1) % LANES // (2 * HL)
    fields, highs, lows, tables_hi, tables_lo = [], [], [], [], []
    for x in range(x_local):
        fields.append(in_ref[:, x].astype(F32).reshape(rows, LANES).astype(BF16))
        pre_grad = out_grad_ref[:, x].astype(F32) * gelu_slope(pre_ref[:, x])
        high, low = split(pre_grad.reshape(rows, LANES))
        ghi_ref[x] = high
        glo_ref[x] = low
        highs.append(high)
        lows.append(low)
        tables_hi.append(jnp.where(lane_x == x, table_hi, 0.0).astype(BF16))
        tables_lo.append(jnp.where(lane_x == x, table_lo, 0.0).astype(BF16))
    field = jnp.concatenate(fields, axis=1)
    high = jnp.concatenate(highs, axis=1)
    low = jnp.concatenate(lows, axis=1)
    table = (jnp.concatenate(tables_hi, axis=0), jnp.concatenate(tables_lo, axis=0))
    raw_in = dot(field, table[0]) + dot(field, table[1])
    raw_grad = product((high, low), table)

    tile = (channels, SUBLANES, LANES)
    sign = jnp.where(iota(tile, 2) % 2 == 0, 1.0, -1.0)
    upper = iota(tile, 1) < y_local

    def joined(raw):
        even = raw[:, :LANES].reshape(tile)
        odd = raw[:, LANES:].reshape(tile)
        return jnp.where(
            upper,
            even + sign * pltpu.roll(even, y_local, 1),
            pltpu.roll(odd, y_local, 1) + sign * odd,
        )

    wide = (channels, SUBLANES, rows)
    row, col = iota(wide, 1), iota(wide, 2)
    gram = dot_rows(field, high) + dot_rows(field, low)
    trace = jnp.where(row == col % SUBLANES, gram.reshape(wide), 0.0)
    trace = jnp.sum(trace, axis=1, keepdims=True)
    at_row = row == col // SUBLANES // x_local
    weight_rows = split(jnp.where(at_row, trace, 0.0).reshape(rows, rows))
    flat = (rows, LANES)
    place = jnp.where(
        iota(flat, 1) == iota(flat, 0) // SUBLANES % x_local * (2 * HL) + HL, 1.0, 0.0
    ).astype(BF16)
    weight_slots = dot(weight_rows[0], place) + dot(weight_rows[1], place)
    ones = jnp.ones((2 * SUBLANES, field.shape[1]), BF16)
    bias = (dot_rows(ones, high) + dot_rows(ones, low))[:SUBLANES]
    bias_rows = split(jnp.where(at_row[0], bias, 0.0))
    bias_slots = dot(bias_rows[0], place) + dot(bias_rows[1], place)
    s_ref[:, 0] = joined(raw_in) + weight_slots.reshape(tile)
    s_ref[:, 1] = joined(raw_grad) + bias_slots[None]


def plane_kernel(r_ref, txh_ref, txl_ref, tyh_ref, tyl_ref, s_ref, stat_ref):
    x_devices, y_devices = s_ref.shape[:2]
    y_local = SUBLANES // 2
    stat_ref[...] = jnp.sum(r_ref[...], axis=0)
    values = jnp.where(slot_mask(y_local), 0.0, r_ref[...])
    values = values.reshape(x_devices, -1, LANES)
    wide = jnp.concatenate([values[g] for g in range(x_devices)], axis=1)
    along_x = product(split(wide), (txh_ref[...], txl_ref[...]))
    lane = iota((along_x.shape[0], LANES), 1)
    sign = jnp.where(lane < LANES // 2, 1.0, -1.0)
    turned = [
        sign * pltpu.roll(along_x[:, g * LANES : (g + 1) * LANES], LANES // 2, 1)
        for g in range(x_devices)
    ]
    both = jnp.concatenate([along_x, jnp.concatenate(turned, axis=1)], axis=0)
    along_y = product((tyh_ref[...], tyl_ref[...]), split(both))
    for g in range(x_devices):
        s_ref[g] = along_y[:, g * LANES : (g + 1) * LANES].reshape(s_ref.shape[1:])


def mode_kernel(cells, r_ref, spread_ref, sum_ref, weight_ref, grad_ref, s_ref):
    channels = sum_ref.shape[0]
    kx_local = weight_ref.shape[0]
    ky = pl.program_id(0)
    half = LANES // 2
    stacked = [
        r_ref[pl.ds(ky * 4 + f * 2 + hh, channels, stride=r_ref.shape[0] // channels), :]
        for hh in range(2)
        for f in range(2)
    ]
    modes = jnp.concatenate(stacked, axis=0).T
    row, lane = iota(modes.shape, 0), iota(modes.shape, 1)
    first = (row % HL == 0) & (lane < half)
    factor = jnp.where(
        lane // channels % 2 == 1, jnp.where(first, 1.0 / cells, 2.0 / cells), 1.0
    )
    modes = modes * factor
    low = modes - modes.astype(BF16).astype(F32)
    left = jnp.concatenate(
        [
            jnp.where(lane < half, modes, pltpu.roll(low, half, 1)),
            jnp.where(lane < half, pltpu.roll(modes, half, 1), low),
        ],
        axis=0,
    ).astype(BF16)
    spread = dot(left, spread_ref[...])
    count = kx_local * HL
    size = channels * channels
    for hh in range(2):
        real = spread[hh * 2 * count : hh * 2 * count + count]
        imag = spread[hh * 2 * count + count : (hh + 1) * 2 * count]
        in_real, in_imag = real[:, :size], imag[:, :size]
        repeat = size // LANES
        grad_real = jnp.concatenate([real[:, size:]] * repeat, axis=1)
        grad_imag = jnp.concatenate([imag[:, size:]] * repeat, axis=1)
        rows = pl.ds(hh * HL, HL)
        tile = (kx_local, HL, size)
        grad_ref[:, 0, 0, rows, :] = (in_real * grad_real + in_imag * grad_imag).reshape(tile)
        grad_ref[:, 0, 1, rows, :] = (in_real * grad_imag - in_imag * grad_real).reshape(tile)
        mix_real = weight_ref[:, 0, 0, rows, :].reshape(count, size)
        mix_imag = weight_ref[:, 0, 1, rows, :].reshape(count, size)
        terms = jnp.concatenate(
            [
                grad_real * mix_real + grad_imag * mix_imag,
                grad_imag * mix_real - grad_real * mix_imag,
            ],
            axis=0,
        )
        high, lower = split(terms)
        back = dot_rows(sum_ref[...], high) + dot_rows(sum_ref[...], lower)
        s_ref[pl.ds(ky * 2 + hh, channels, stride=SUBLANES), :] = back


def inverse_kernel(r_ref, stat_ref, tyh_ref, tyl_ref, txh_ref, txl_ref, s_ref):
    x_devices, y_devices = s_ref.shape[:2]
    y_local = SUBLANES // 2
    values = r_ref[...].reshape(x_devices, y_devices * SUBLANES, LANES)
    lane = iota(values.shape[1:], 1)
    sign = jnp.where(lane < LANES // 2, -1.0, 1.0)
    wide = jnp.concatenate([values[g] for g in range(x_devices)], axis=1)
    turned = [sign * pltpu.roll(values[g], LANES // 2, 1) for g in range(x_devices)]
    both = jnp.concatenate([wide, jnp.concatenate(turned, axis=1)], axis=0)
    along_y = product((tyh_ref[...], tyl_ref[...]), split(both))
    along_x = product(split(along_y), (txh_ref[...], txl_ref[...]), dot_rows)
    slots = slot_mask(y_local)
    for g in range(x_devices):
        block = along_x[:, g * LANES : (g + 1) * LANES].reshape(s_ref.shape[1:])
        s_ref[g] = jnp.where(slots, stat_ref[0], block)


def result_kernel(
    scale, r_ref, stat_ref, hi_ref, lo_ref, kw_ref, ghi_ref, glo_ref, grad_ref, point_ref, bias_ref
):
    channels, x_block = grad_ref.shape[:2]
    y_local = SUBLANES // 2
    x_local = LANES // (2 * HL)
    step = pl.program_id(0)
    rows = channels * SUBLANES
    tile = (channels, SUBLANES, LANES)
    values = r_ref[...].reshape(tile)
    turned = pltpu.roll(values, y_local, 1)
    sign = jnp.where(iota(tile, 2) % 2 == 0, 1.0, -1.0)
    upper = iota(tile, 1) < y_local
    left = jnp.concatenate(
        [
            jnp.where(upper, values, sign * turned).reshape(rows, LANES),
            jnp.where(upper, turned, sign * values).reshape(rows, LANES),
        ],
        axis=1,
    )
    high, low = split(left)
    kw_high, kw_low = split(kw_ref[...])
    left = jnp.concatenate([high, low, high, kw_high, kw_high, kw_low], axis=1)
    table_hi = hi_ref[...].astype(F32)
    table_lo = lo_ref[...].astype(F32)
    row_x = iota(table_hi.shape, 0) % LANES // (2 * HL)
    for k in range(x_block):
        keep = row_x == step * x_block + k
        t_hi = jnp.where(keep, table_hi, 0.0).astype(BF16)
        t_lo = jnp.where(keep, table_lo, 0.0).astype(BF16)
        right = jnp.concatenate([t_hi, t_hi, t_lo, ghi_ref[k], glo_ref[k], ghi_ref[k]], axis=0)
        grad_ref[:, k] = dot(left, right).reshape(tile)

    @pl.when(step == 0)
    def _():
        flat = (LANES, channels)
        lane, out = iota(flat, 0), iota(flat, 1)
        point = jnp.zeros(point_ref.shape, F32)
        bias = jnp.zeros(bias_ref.shape, F32)
        for y in range(y_local):
            place = (lane == out % x_local * (2 * HL) + HL) & (out // x_local == y)
            place = jnp.where(place, 1.0, 0.0)
            taken = r_ref[pl.ds(y, channels, stride=SUBLANES), :]
            point += jnp.dot(
                taken, place, precision=HIGHEST_PRECISION, preferred_element_type=F32
            )
            taken = jnp.broadcast_to(stat_ref[1, pl.ds(y, 1), :], (SUBLANES, LANES))
            bias += jnp.dot(
                taken, place, precision=HIGHEST_PRECISION, preferred_element_type=F32
            )
        point_ref[...] = point * scale
        bias_ref[...] = bias * scale


def call(kernel, out_shape, name, **options):
    params = pltpu.CompilerParams(vmem_limit_bytes=56 << 20)
    return pl.pallas_call(
        kernel, out_shape=out_shape, name=name, compiler_params=params, **options
    )


def whole(shape):
    zeros = (0,) * len(shape)
    return pl.BlockSpec(shape, lambda *_: zeros)


def to_tiles(array):
    lead, (rows, depth) = array.shape[:-2], array.shape[-2:]
    split_up = array.reshape(lead + (rows, depth // LANES, LANES))
    return jnp.swapaxes(split_up, -3, -2).reshape(lead + (SUBLANES, LANES))


def from_tiles(array, rows, depth):
    lead = array.shape[:-2]
    split_up = array.reshape(lead + (depth // LANES, rows, LANES))
    return jnp.swapaxes(split_up, -3, -2).reshape(lead + (rows, depth))


def transposed(inputs, pre_act, grad_out, point_weight, mode_weight):
    channels, x_local, y_local, depth = inputs.shape
    kx_local, ky_local, _, kz_count, pairs = mode_weight.shape
    x_devices = lax.axis_size("gx")
    y_devices = lax.axis_size("gy")
    devices = x_devices * y_devices
    hh_count = kz_count // HL
    cells = x_local * x_devices * y_local * y_devices * depth
    scale = 1.0 / math.sqrt(cells)
    axes = ("gx", "gy")
    rows = channels * SUBLANES

    def struct(shape, kind=F32):
        return jax.ShapeDtypeStruct(shape, kind)

    def exchange(chunks):
        return lax.all_to_all(chunks, axes, 0, 0)

    z_high, z_low = split_table(depth_table(depth, kz_count, x_local))
    tx = split_table(x_table(x_devices, x_local, kx_local))
    ty = split_table(y_table(y_devices, y_local, ky_local, hh_count))
    tyi = split_table(y_inverse_table(y_devices, y_local, ky_local, hh_count))
    spread = spread_table(channels)
    summed = np.repeat(np.eye(channels), channels, axis=1).astype(BF16)

    chunks, g_high, g_low = call(
        grid_kernel,
        (
            struct((channels, 2, SUBLANES, LANES)),
            struct((x_local, rows, LANES), BF16),
            struct((x_local, rows, LANES), BF16),
        ),
        "grid",
    )(to_tiles(inputs), to_tiles(pre_act), to_tiles(grad_out), z_high, z_low)
    planes = exchange(chunks)
    mode_rows = ky_local * 2 * hh_count
    chunks, stats = call(
        plane_kernel,
        (struct((x_devices, y_devices, mode_rows, LANES)), struct((2, SUBLANES, LANES))),
        "plane",
    )(planes, *tx, *ty)
    modes = exchange(chunks.reshape(devices, mode_rows, LANES))
    block = (kx_local, 1, 2, kz_count, pairs)
    block_spec = pl.BlockSpec(block, lambda k: (0, k, 0, 0, 0))
    mode_grad, chunks = call(
        lambda *refs: mode_kernel(cells, *refs),
        (struct(mode_weight.shape), struct((devices * SUBLANES, LANES))),
        "mode",
        grid=(ky_local,),
        in_specs=[
            whole((devices * mode_rows, LANES)),
            whole(spread.shape),
            whole(summed.shape),
            block_spec,
        ],
        out_specs=(block_spec, whole((devices * SUBLANES, LANES))),
    )(modes.reshape(devices * mode_rows, LANES), spread, summed, mode_weight)
    back = exchange(chunks.reshape(devices, SUBLANES, LANES))
    chunks = call(
        inverse_kernel, struct((x_devices, y_devices, SUBLANES, LANES)), "inverse"
    )(back, stats, *tyi, *tx)
    near = exchange(chunks.reshape(devices, SUBLANES, LANES))
    kron = (
        point_weight[:, None, :, None] * jnp.eye(SUBLANES, dtype=F32)[None, :, None, :]
    ).reshape(rows, rows)
    x_block = max(x_local // 4, 1)
    g_spec = pl.BlockSpec((x_block, rows, LANES), lambda k: (k, 0, 0))
    grad, point_grad, bias_grad = call(
        lambda *refs: result_kernel(scale, *refs),
        (
            struct((channels, x_local, SUBLANES, LANES)),
            struct((channels, channels)),
            struct((SUBLANES, channels)),
        ),
        "result",
        grid=(x_local // x_block,),
        in_specs=[
            whole((rows, LANES)),
            whole((2, SUBLANES, LANES)),
            whole((2 * LANES, LANES)),
            whole((2 * LANES, LANES)),
            whole((rows, rows)),
            g_spec,
            g_spec,
        ],
        out_specs=(
            pl.BlockSpec((channels, x_block, SUBLANES, LANES), lambda k: (0, k, 0, 0)),
            whole((channels, channels)),
            whole((SUBLANES, channels)),
        ),
    )(near.reshape(rows, LANES), stats, z_high.T, z_low.T, kron, g_high, g_low)
    return (from_tiles(grad, y_local, depth), point_grad, bias_grad[0], mode_grad)


def one_channel_each(inputs, mode_weight):
    channels, x_local, y_local, depth = inputs.shape
    kx_local, ky_local, _, kz_count, _ = mode_weight.shape
    return (
        channels == lax.axis_size("gx") * lax.axis_size("gy")
        and LANES % channels == 0
        and depth == 2 * LANES
        and y_local * 2 == SUBLANES
        and kz_count == 2 * HL
        and ky_local * 2 == SUBLANES
        and x_local * 2 * HL == LANES
        and kx_local == x_local
        and x_local * y_local == channels
    )


def shards(inputs, pre_act, grad_out, point_weight, mode_weight):
    plan = transposed if one_channel_each(inputs, mode_weight) else partial_sums
    return plan(inputs, pre_act, grad_out, point_weight, mode_weight)


def solution(mesh):
    return jax.shard_map(
        shards,
        mesh=mesh,
        in_specs=(
            P(None, "gx", "gy", None),
            P(None, "gx", "gy", None),
            P(None, "gx", "gy", None),
            P(),
            P("gx", "gy", None, None, None),
        ),
        out_specs=(P(None, "gx", "gy", None), P(), P(), P("gx", "gy", None, None, None)),
        check_vma=False,
    )
```

profile of v0, /device:TPU:0, one launch (start us, length us, event | category | flops | bytes accessed | tf_op | source)
XLA Modules:
  0.0 78.0 jit_solution(8659966283329931614)
XLA Ops:
  0.6 4.4 %grid.1 = (f32[32,2,8,128]{3,2,1,0:T(8,128)}, bf16[8,256,128]{2,1,0:T(8,128)(2,1)}, bf16[8,256,128]{2,1,0:T(8,128)(2,1)}) custom-call(bf16[32,8,8,128]{3,2,1,0:T(8,128)(2,1)} %bitcast.31, bf16[32,8,8,128]{3,2,1,0:T(8,128)(2,1)} %bitcast.32, bf16[32,8,8,128]{3,2,1,0:T(8,128)(2,1)} %bitcast.33, bf16[128,256]{1,0:T(8,128)(2,1)} %constant.24.clone.hi_ref, ...), custom_call_target="tpu_custom_call" | custom-call | tf_op jit(solution)/shard_map/grid/pallas_call | solution.py:575
  5.1 17.4 %all_to_all.20.r_ref = f32[32,2,8,128]{3,2,1,0:T(8,128)} all-to-all(f32[32,2,8,128]{3,2,1,0:T(8,128)} %get-tuple-element.14), channel_id=1, replica_groups=mesh['gx'=4,'gy'=8] {'gx','gy'}, dimensions={0} | all-to-all | bytes 524288 | tf_op jit(solution)/shard_map/all_to_all | solution.py:566
  22.5 0.0 copy-start.2
  22.5 2.7 %plane.1 = (f32[4,8,16,128]{3,2,1,0:T(8,128)}, f32[2,8,128]{2,1,0:T(8,128)}) custom-call(f32[32,2,8,128]{3,2,1,0:T(8,128)} %all_to_all.20.r_ref, bf16[512,512]{1,0:T(8,128)(2,1)} %constant.26.clone.txh_ref, bf16[512,512]{1,0:T(8,128)(2,1)} %constant.27.clone.txl_ref, bf16[128,256]{1,0:T(8,128)(2,1)} %constant.28.clone.tyh_ref, ...), custom_call_target="tpu_custom_call" | custom-call | tf_op jit(solution)/shard_map/plane/pallas_call | solution.py:586
  25.3 13.3 %all_to_all.21 = f32[32,16,128]{2,1,0:T(8,128)} all-to-all(f32[32,16,128]{2,1,0:T(8,128)} %bitcast.35), channel_id=1, replica_groups=mesh['gx'=4,'gy'=8] {'gx','gy'}, dimensions={0} | all-to-all | bytes 524288 | tf_op jit(solution)/shard_map/all_to_all | solution.py:566
  38.5 7.2 %mode.1 = (f32[8,4,2,16,1024]{4,3,2,1,0:T(8,128)}, f32[256,128]{1,0:T(8,128)}) custom-call(f32[512,128]{1,0:T(8,128)} %bitcast.29, bf16[128,1152]{1,0:T(8,128)(2,1)} %constant.30.clone.refs_1_, bf16[32,1024]{1,0:T(8,128)(2,1)} %constant.31.clone.refs_2_, f32[8,4,2,16,1024]{4,3,2,1,0:T(8,128)} %refs_3_.2), custom_call_target="tpu_custom_call" | custom-call | tf_op jit(solution)/shard_map/mode/pallas_call | solution.py:594
  45.7 2.8 %all-to-all-start.2 = ((f32[32,8,128]{2,1,0:T(8,128)}), f32[32,8,128]{2,1,0:T(8,128)S(1)}, u32[]{:S(2)}, u32[]{:S(2)}) async-start(f32[32,8,128]{2,1,0:T(8,128)} %bitcast.36), calls=%async_computation.2 | async-start | bytes 262144 | tf_op jit(solution)/shard_map/all_to_all | solution.py:566
  48.5 8.1 %all-to-all-done.2.r_ref = f32[32,8,128]{2,1,0:T(8,128)S(1)} async-done(((f32[32,8,128]{2,1,0:T(8,128)}), f32[32,8,128]{2,1,0:T(8,128)S(1)}, u32[]{:S(2)}, u32[]{:S(2)}) %all-to-all-start.2) | async-done | bytes 131104 | tf_op jit(solution)/shard_map/all_to_all | solution.py:566
  56.6 0.0 copy-start.1
  56.7 0.7 copy-done.1
  57.3 2.8 %inverse.1 = f32[4,8,8,128]{3,2,1,0:T(8,128)} custom-call(f32[32,8,128]{2,1,0:T(8,128)} %copy-done.1, f32[2,8,128]{2,1,0:T(8,128)} %get-tuple-element.17.stat_ref.refs_1_, bf16[64,128]{1,0:T(8,128)(2,1)} %constant.32.clone.tyh_ref, bf16[64,128]{1,0:T(8,128)(2,1)} %constant.33.clone.tyl_ref, bf16[512,512]{1,0:T(8,128)(2,1)} %constant.26.clone.txh_ref, ...), custom_call_target="tpu_custom_call" | custom-call | tf_op jit(solution)/shard_map/inverse/pallas_call | solution.py:608
  60.1 2.6 %all-to-all-start.3 = ((f32[32,8,128]{2,1,0:T(8,128)}), f32[32,8,128]{2,1,0:T(8,128)S(1)}, u32[]{:S(2)}, u32[]{:S(2)}) async-start(f32[32,8,128]{2,1,0:T(8,128)} %bitcast.34), calls=%async_computation.3 | async-start | bytes 262144 | tf_op jit(solution)/shard_map/all_to_all | solution.py:566
  62.7 0.0 copy-done.2
  62.7 2.5 %broadcast_multiply_fusion = f32[32,8,32,8]{3,2,1,0:T(8,128)} fusion(f32[8,8]{1,0:T(8,128)S(1)} %fusion, f32[32,32]{1,0:T(8,128)S(1)} %copy-done.2), kind=kLoop, calls=%fused_computation | loop fusion | flops 65536 | bytes 266496 | tf_op jit(solution)/shard_map/mul | solution.py:613
  65.2 4.7 %mul.20.refs_4_ = f32[256,256]{1,0:T(8,128)} reshape(f32[32,8,32,8]{3,2,1,0:T(8,128)} %broadcast_multiply_fusion) | data formatting | bytes 524288 | tf_op jit(solution)/shard_map/mul | solution.py:613
  69.9 0.9 %all-to-all-done.3 = f32[32,8,128]{2,1,0:T(8,128)S(1)} async-done(((f32[32,8,128]{2,1,0:T(8,128)}), f32[32,8,128]{2,1,0:T(8,128)S(1)}, u32[]{:S(2)}, u32[]{:S(2)}) %all-to-all-start.3) | async-done | bytes 131104 | tf_op jit(solution)/shard_map/all_to_all | solution.py:566
  70.8 0.0 copy-start
  70.8 0.6 copy-done
  71.5 5.3 %result.1 = (f32[32,8,8,128]{3,2,1,0:T(8,128)}, f32[32,32]{1,0:T(8,128)}, f32[8,32]{1,0:T(8,128)}) custom-call(f32[256,128]{1,0:T(8,128)} %bitcast.30, f32[2,8,128]{2,1,0:T(8,128)} %get-tuple-element.17.stat_ref.refs_1_, bf16[256,128]{1,0:T(8,128)(2,1)} %constant.34.clone.refs_2_, bf16[256,128]{1,0:T(8,128)(2,1)} %constant.35.clone.refs_3_, ...), custom_call_target="tpu_custom_call" | custom-call | tf_op jit(solution)/shard_map/result/pallas_call | solution.py:617
  76.8 1.2 %slice_bitcast_fusion = f32[32]{0:T(128)} fusion(f32[8,32]{1,0:T(8,128)} %get-tuple-element.22), kind=kLoop, calls=%fused_computation.3 | loop fusion | bytes 256 | tf_op jit(solution)/shard_map/squeeze | solution.py:641
  (1 shorter events, 0.0 us)
Async XLA Ops:
  22.5 40.1 %copy-start.2 = (f32[32,32]{1,0:T(8,128)S(1)}, f32[32,32]{1,0:T(8,128)}, u32[]{:S(2)}) copy-start(f32[32,32]{1,0:T(8,128)} %param.20) | copy-start | bytes 12292
  45.7 10.9 %all-to-all-start.2 = ((f32[32,8,128]{2,1,0:T(8,128)}), f32[32,8,128]{2,1,0:T(8,128)S(1)}, u32[]{:S(2)}, u32[]{:S(2)}) async-start(f32[32,8,128]{2,1,0:T(8,128)} %bitcast.36), calls=%async_computation.2 | async-start | bytes 262144 | tf_op jit(solution)/shard_map/all_to_all | solution.py:566
  56.6 0.7 copy-start.1
  60.1 10.7 %all-to-all-start.3 = ((f32[32,8,128]{2,1,0:T(8,128)}), f32[32,8,128]{2,1,0:T(8,128)S(1)}, u32[]{:S(2)}, u32[]{:S(2)}) async-start(f32[32,8,128]{2,1,0:T(8,128)} %bitcast.34), calls=%async_computation.3 | async-start | bytes 262144 | tf_op jit(solution)/shard_map/all_to_all | solution.py:566
  70.8 0.6 copy-start
where the time goes:
time: 78.6 us; the launch traced here: 78 us
  blocking collectives  30.7 us (39%)
  Pallas kernels  22.4 us (28%)
  waiting for transfers between devices  9.05 us (12%)
  local copies, waits for them, and re-layouts  7.18 us (9%)
  starting transfers between devices  5.34 us (7%)
  other arithmetic  2.55 us (3%)
    all_to_all x2, blocking collectives, exchange(): return lax.all_to_all(chunks, axes, 0, 0)  30.7 us
    all_to_all x2, waiting for transfers between devices, exchange(): return lax.all_to_all(chunks, axes, 0, 0)  9.05 us
    pallas_call x1, Pallas kernels, transposed(): call(lambda *refs: mode_kernel(cells, *refs), (struct(mode_weight.shape),...  7.16 us
    all_to_all x2, starting transfers between devices, exchange(): return lax.all_to_all(chunks, axes, 0, 0)  5.34 us
    pallas_call x1, Pallas kernels, transposed(): call(lambda *refs: result_kernel(scale, *refs), (struct((channels, x_loca...  5.32 us
    mul x1, local copies, waits for them, and re-layouts, transposed(): point_weight[:, None, :, None]  4.7 us
    pallas_call x1, Pallas kernels, transposed(): call(grid_kernel, (struct((channels, 2, SUBLANES, LANES)), struct((x_loca...  4.44 us
    pallas_call x1, Pallas kernels, transposed(): call(inverse_kernel, struct((x_devices, y_devices, SUBLANES, LANES)), 'in...  2.78 us
  transfers between devices with their start and end apart: 2, of which 2 were waited for; matrix products, arithmetic and copies ran while one was open for 9% of the time, Pallas kernels for 0%

commit v1 on v0

--- a/solution.py
+++ b/solution.py
@@ -1,3 +1,4 @@
+import functools
 import math
 
 import jax
@@ -321,22 +322,49 @@
     return (iota(shape, 0) < y_local) & (iota(shape, 1) % (2 * HL) == HL)
 
 
-def grid_kernel(in_ref, pre_ref, out_grad_ref, hi_ref, lo_ref, s_ref, ghi_ref, glo_ref):
+def grid_kernel(count, *refs):
+    in_hbm, pre_hbm, out_grad_hbm, hi_hbm, lo_hbm = refs[:5]
+    later_hbm, refs = refs[5 : 5 + count], refs[5 + count :]
+    s_ref, ghi_ref, glo_ref = refs[:3]
+    later, refs = refs[3 : 3 + count], refs[3 + count :]
+    in_ref, pre_ref, out_grad_ref, hi_ref, lo_ref, near_sems, far_sems = refs
     channels, x_local = in_ref.shape[:2]
     y_local = SUBLANES // 2
     rows = channels * SUBLANES
-    table_hi = hi_ref[...].astype(F32)
-    table_lo = lo_ref[...].astype(F32)
-    lane_x = iota(table_hi.shape, 1) % LANES // (2 * HL)
+    step = max(x_local // 4, 1)
+    parts = {}
+    for x in range(0, x_local, step):
+        at = (slice(None), pl.ds(x, step))
+        for index, pair in enumerate(((pre_hbm, pre_ref), (out_grad_hbm, out_grad_ref))):
+            sem = near_sems.at[2 * (x // step) + index]
+            parts[x, index] = pltpu.make_async_copy(pair[0].at[at], pair[1].at[at], sem)
+            parts[x, index].start()
+    whole_copies = [(in_hbm, in_ref), (hi_hbm, hi_ref), (lo_hbm, lo_ref)]
+    whole_copies = whole_copies + list(zip(later_hbm, later))
+    whole_copies = [
+        pltpu.make_async_copy(source, target, far_sems.at[index])
+        for index, (source, target) in enumerate(whole_copies)
+    ]
+    for copy in whole_copies:
+        copy.start()
     fields, highs, lows, tables_hi, tables_lo = [], [], [], [], []
     for x in range(x_local):
-        fields.append(in_ref[:, x].astype(F32).reshape(rows, LANES).astype(BF16))
+        if x % step == 0:
+            parts[x, 0].wait()
+            parts[x, 1].wait()
         pre_grad = out_grad_ref[:, x].astype(F32) * gelu_slope(pre_ref[:, x])
         high, low = split(pre_grad.reshape(rows, LANES))
         ghi_ref[x] = high
         glo_ref[x] = low
         highs.append(high)
         lows.append(low)
+    for copy in whole_copies[:3]:
+        copy.wait()
+    table_hi = hi_ref[...].astype(F32)
+    table_lo = lo_ref[...].astype(F32)
+    lane_x = iota(table_hi.shape, 1) % LANES // (2 * HL)
+    for x in range(x_local):
+        fields.append(in_ref[:, x].astype(F32).reshape(rows, LANES).astype(BF16))
         tables_hi.append(jnp.where(lane_x == x, table_hi, 0.0).astype(BF16))
         tables_lo.append(jnp.where(lane_x == x, table_lo, 0.0).astype(BF16))
     field = jnp.concatenate(fields, axis=1)
@@ -377,12 +405,33 @@
     bias_slots = dot(bias_rows[0], place) + dot(bias_rows[1], place)
     s_ref[:, 0] = joined(raw_in) + weight_slots.reshape(tile)
     s_ref[:, 1] = joined(raw_grad) + bias_slots[None]
-
-
-def plane_kernel(r_ref, txh_ref, txl_ref, tyh_ref, tyl_ref, s_ref, stat_ref):
+    for copy in whole_copies[3:]:
+        copy.wait()
+
+
+def slot_place(channels, x_local, y):
+    lane, out = iota((LANES, channels), 0), iota((LANES, channels), 1)
+    place = (lane == out % x_local * (2 * HL) + HL) & (out // x_local == y)
+    return jnp.where(place, 1.0, 0.0)
+
+
+def from_slots(taken, place):
+    return jnp.dot(taken, place, precision=HIGHEST_PRECISION, preferred_element_type=F32)
+
+
+def plane_kernel(
+    scale, r_ref, txh_ref, txl_ref, tyh_ref, tyl_ref, s_ref, stat_ref, bias_ref
+):
     x_devices, y_devices = s_ref.shape[:2]
     y_local = SUBLANES // 2
-    stat_ref[...] = jnp.sum(r_ref[...], axis=0)
+    stats = jnp.sum(r_ref[...], axis=0)
+    stat_ref[...] = stats[0]
+    channels = bias_ref.shape[1]
+    bias = jnp.zeros((SUBLANES, channels), F32)
+    for y in range(y_local):
+        row = jnp.where(iota((SUBLANES, LANES), 0) == y, stats[1], 0.0)
+        bias += from_slots(row, slot_place(channels, channels // y_local, y))
+    bias_ref[...] = jnp.sum(bias, axis=0, keepdims=True) * scale
     values = jnp.where(slot_mask(y_local), 0.0, r_ref[...])
     values = values.reshape(x_devices, -1, LANES)
     wide = jnp.concatenate([values[g] for g in range(x_devices)], axis=1)
@@ -399,17 +448,59 @@
         s_ref[g] = along_y[:, g * LANES : (g + 1) * LANES].reshape(s_ref.shape[1:])
 
 
-def mode_kernel(cells, r_ref, spread_ref, sum_ref, weight_ref, grad_ref, s_ref):
-    channels = sum_ref.shape[0]
-    kx_local = weight_ref.shape[0]
+def mode_rows(r_ref, picks, channels):
+    stride = r_ref.shape[0] // channels
+    taken = [r_ref[pl.ds(pick, channels, stride=stride), :] for pick in picks]
+    return jnp.concatenate(taken, axis=0).T
+
+
+def repeated(values, times):
+    return jnp.concatenate([values] * times, axis=1)
+
+
+def back_kernel(cells, channels, r_ref, weight_ref, s_ref):
+    size = channels * channels
+    kx_local, ky_local = weight_ref.shape[:2]
+    shape = (channels, size)
+    sums = jnp.where(iota(shape, 0) == iota(shape, 1) // channels, 1.0, 0.0).astype(BF16)
+    count = kx_local * HL
+    times = size // LANES
+    group = LANES // channels // 2
+    for start in range(0, ky_local, group):
+        places = [(ky, hh) for ky in range(start, start + group) for hh in range(2)]
+        modes = mode_rows(r_ref, [ky * 4 + 2 + hh for ky, hh in places], channels)
+        row, lane = iota(modes.shape, 0), iota(modes.shape, 1)
+        first = (row % HL == 0) & (lane // channels % 2 == 0)
+        modes = modes * jnp.where(first, 1.0 / cells, 2.0 / cells)
+        for index, (ky, hh) in enumerate(places):
+            grad = jnp.where(lane // channels == index, modes, 0.0)
+            shift = channels
+            while shift < LANES:
+                grad = grad + pltpu.roll(grad, shift, 1)
+                shift = shift * 2
+            grad_real, grad_imag = repeated(grad[:count], times), repeated(grad[count:], times)
+            rows = slice(hh * HL, (hh + 1) * HL)
+            mix_real = weight_ref[:, ky, 0, rows, :].reshape(count, size)
+            mix_imag = weight_ref[:, ky, 1, rows, :].reshape(count, size)
+            terms = jnp.concatenate(
+                [
+                    grad_real * mix_real + grad_imag * mix_imag,
+                    grad_imag * mix_real - grad_real * mix_imag,
+                ],
+                axis=0,
+            )
+            high, low = split(terms)
+            back = dot_rows(sums, high) + dot_rows(sums, low)
+            s_ref[pl.ds(ky * 2 + hh, channels, stride=SUBLANES), :] = back
+
+
+def outer_kernel(cells, r_ref, spread_ref, grad_ref):
+    kx_local = grad_ref.shape[0]
+    size = grad_ref.shape[-1]
+    channels = spread_ref.shape[0] // 4
     ky = pl.program_id(0)
     half = LANES // 2
-    stacked = [
-        r_ref[pl.ds(ky * 4 + f * 2 + hh, channels, stride=r_ref.shape[0] // channels), :]
-        for hh in range(2)
-        for f in range(2)
-    ]
-    modes = jnp.concatenate(stacked, axis=0).T
+    modes = mode_rows(r_ref, [ky * 4 + f * 2 + hh for hh in range(2) for f in range(2)], channels)
     row, lane = iota(modes.shape, 0), iota(modes.shape, 1)
     first = (row % HL == 0) & (lane < half)
     factor = jnp.where(
@@ -426,30 +517,40 @@
     ).astype(BF16)
     spread = dot(left, spread_ref[...])
     count = kx_local * HL
-    size = channels * channels
     for hh in range(2):
         real = spread[hh * 2 * count : hh * 2 * count + count]
         imag = spread[hh * 2 * count + count : (hh + 1) * 2 * count]
         in_real, in_imag = real[:, :size], imag[:, :size]
-        repeat = size // LANES
-        grad_real = jnp.concatenate([real[:, size:]] * repeat, axis=1)
-        grad_imag = jnp.concatenate([imag[:, size:]] * repeat, axis=1)
+        times = size // LANES
+        grad_real, grad_imag = repeated(real[:, size:], times), repeated(imag[:, size:], times)
         rows = pl.ds(hh * HL, HL)
         tile = (kx_local, HL, size)
         grad_ref[:, 0, 0, rows, :] = (in_real * grad_real + in_imag * grad_imag).reshape(tile)
         grad_ref[:, 0, 1, rows, :] = (in_real * grad_imag - in_imag * grad_real).reshape(tile)
-        mix_real = weight_ref[:, 0, 0, rows, :].reshape(count, size)
-        mix_imag = weight_ref[:, 0, 1, rows, :].reshape(count, size)
-        terms = jnp.concatenate(
-            [
-                grad_real * mix_real + grad_imag * mix_imag,
-                grad_imag * mix_real - grad_real * mix_imag,
-            ],
-            axis=0,
-        )
-        high, lower = split(terms)
-        back = dot_rows(sum_ref[...], high) + dot_rows(sum_ref[...], lower)
-        s_ref[pl.ds(ky * 2 + hh, channels, stride=SUBLANES), :] = back
+
+
+def local_kernel(weight_ref, ghi_ref, glo_ref, local_ref):
+    channels, x_local = local_ref.shape[:2]
+    rows = channels * SUBLANES
+    spread = jnp.where(
+        iota((rows, channels), 0) // SUBLANES == iota((rows, channels), 1), 1.0, 0.0
+    )
+    tall = jnp.dot(
+        spread, weight_ref[...], precision=HIGHEST_PRECISION, preferred_element_type=F32
+    )
+    square = lax.dot_general(
+        tall,
+        spread,
+        (((1,), (1,)), ((), ())),
+        precision=HIGHEST_PRECISION,
+        preferred_element_type=F32,
+    )
+    same = iota(square.shape, 0) % SUBLANES == iota(square.shape, 1) % SUBLANES
+    high, low = split(jnp.where(same, square, 0.0))
+    left = jnp.concatenate([high, high, low], axis=1)
+    for x in range(x_local):
+        right = jnp.concatenate([ghi_ref[x], glo_ref[x], ghi_ref[x]], axis=0)
+        local_ref[:, x] = dot(left, right).reshape(channels, SUBLANES, LANES)
 
 
 def inverse_kernel(r_ref, stat_ref, tyh_ref, tyl_ref, txh_ref, txl_ref, s_ref):
@@ -466,73 +567,58 @@
     slots = slot_mask(y_local)
     for g in range(x_devices):
         block = along_x[:, g * LANES : (g + 1) * LANES].reshape(s_ref.shape[1:])
-        s_ref[g] = jnp.where(slots, stat_ref[0], block)
-
-
-def result_kernel(
-    scale, r_ref, stat_ref, hi_ref, lo_ref, kw_ref, ghi_ref, glo_ref, grad_ref, point_ref, bias_ref
-):
+        s_ref[g] = jnp.where(slots, stat_ref[...], block)
+
+
+def result_kernel(scale, r_ref, hi_ref, lo_ref, local_ref, grad_ref, point_ref, left_ref):
     channels, x_block = grad_ref.shape[:2]
     y_local = SUBLANES // 2
     x_local = LANES // (2 * HL)
     step = pl.program_id(0)
     rows = channels * SUBLANES
     tile = (channels, SUBLANES, LANES)
-    values = r_ref[...].reshape(tile)
-    turned = pltpu.roll(values, y_local, 1)
-    sign = jnp.where(iota(tile, 2) % 2 == 0, 1.0, -1.0)
-    upper = iota(tile, 1) < y_local
-    left = jnp.concatenate(
-        [
-            jnp.where(upper, values, sign * turned).reshape(rows, LANES),
-            jnp.where(upper, turned, sign * values).reshape(rows, LANES),
-        ],
-        axis=1,
-    )
-    high, low = split(left)
-    kw_high, kw_low = split(kw_ref[...])
-    left = jnp.concatenate([high, low, high, kw_high, kw_high, kw_low], axis=1)
+
+    @pl.when(step == 0)
+    def _():
+        values = r_ref[...].reshape(tile)
+        turned = pltpu.roll(values, y_local, 1)
+        sign = jnp.where(iota(tile, 2) % 2 == 0, 1.0, -1.0)
+        upper = iota(tile, 1) < y_local
+        left = jnp.concatenate(
+            [
+                jnp.where(upper, values, sign * turned).reshape(rows, LANES),
+                jnp.where(upper, turned, sign * values).reshape(rows, LANES),
+            ],
+            axis=1,
+        )
+        high, low = split(left)
+        left_ref[...] = jnp.concatenate([high, low, high], axis=1)
+        point = jnp.zeros(point_ref.shape, F32)
+        for y in range(y_local):
+            taken = r_ref[pl.ds(y, channels, stride=SUBLANES), :]
+            point += from_slots(taken, slot_place(channels, x_local, y))
+        point_ref[...] = point * scale
+
     table_hi = hi_ref[...].astype(F32)
     table_lo = lo_ref[...].astype(F32)
     row_x = iota(table_hi.shape, 0) % LANES // (2 * HL)
     for k in range(x_block):
-        keep = row_x == step * x_block + k
-        t_hi = jnp.where(keep, table_hi, 0.0).astype(BF16)
-        t_lo = jnp.where(keep, table_lo, 0.0).astype(BF16)
-        right = jnp.concatenate([t_hi, t_hi, t_lo, ghi_ref[k], glo_ref[k], ghi_ref[k]], axis=0)
-        grad_ref[:, k] = dot(left, right).reshape(tile)
-
-    @pl.when(step == 0)
-    def _():
-        flat = (LANES, channels)
-        lane, out = iota(flat, 0), iota(flat, 1)
-        point = jnp.zeros(point_ref.shape, F32)
-        bias = jnp.zeros(bias_ref.shape, F32)
-        for y in range(y_local):
-            place = (lane == out % x_local * (2 * HL) + HL) & (out // x_local == y)
-            place = jnp.where(place, 1.0, 0.0)
-            taken = r_ref[pl.ds(y, channels, stride=SUBLANES), :]
-            point += jnp.dot(
-                taken, place, precision=HIGHEST_PRECISION, preferred_element_type=F32
-            )
-            taken = jnp.broadcast_to(stat_ref[1, pl.ds(y, 1), :], (SUBLANES, LANES))
-            bias += jnp.dot(
-                taken, place, precision=HIGHEST_PRECISION, preferred_element_type=F32
-            )
-        point_ref[...] = point * scale
-        bias_ref[...] = bias * scale
-
-
-def call(kernel, out_shape, name, **options):
-    params = pltpu.CompilerParams(vmem_limit_bytes=56 << 20)
+        x = step * x_block + k
+        t_hi = jnp.where(row_x == x, table_hi, 0.0).astype(BF16)
+        t_lo = jnp.where(row_x == x, table_lo, 0.0).astype(BF16)
+        right = jnp.concatenate([t_hi, t_hi, t_lo], axis=0)
+        grad_ref[:, k] = dot(left_ref[...], right).reshape(tile) + local_ref[:, x]
+
+
+def call(kernel, out_shape, name, vmem=16, **options):
+    params = pltpu.CompilerParams(vmem_limit_bytes=vmem << 20)
     return pl.pallas_call(
         kernel, out_shape=out_shape, name=name, compiler_params=params, **options
     )
 
 
-def whole(shape):
-    zeros = (0,) * len(shape)
-    return pl.BlockSpec(shape, lambda *_: zeros)
+def held(count):
+    return [pl.BlockSpec(memory_space=pltpu.VMEM)] * count
 
 
 def to_tiles(array):
@@ -570,74 +656,102 @@
     ty = split_table(y_table(y_devices, y_local, ky_local, hh_count))
     tyi = split_table(y_inverse_table(y_devices, y_local, ky_local, hh_count))
     spread = spread_table(channels)
-    summed = np.repeat(np.eye(channels), channels, axis=1).astype(BF16)
-
-    chunks, g_high, g_low = call(
-        grid_kernel,
+
+    field_shape = (channels, x_local, SUBLANES, LANES)
+    later = (*tx, *ty, *tyi, z_high.T, z_low.T, mode_weight)
+    chunks, g_high, g_low, *later = call(
+        functools.partial(grid_kernel, len(later)),
         (
             struct((channels, 2, SUBLANES, LANES)),
             struct((x_local, rows, LANES), BF16),
             struct((x_local, rows, LANES), BF16),
+            *(struct(array.shape, array.dtype) for array in later),
         ),
         "grid",
-    )(to_tiles(inputs), to_tiles(pre_act), to_tiles(grad_out), z_high, z_low)
+        vmem=24,
+        in_specs=[pl.BlockSpec(memory_space=pltpu.HBM)] * (5 + len(later)),
+        out_specs=held(3 + len(later)),
+        scratch_shapes=[
+            *([pltpu.VMEM(field_shape, BF16)] * 3),
+            *([pltpu.VMEM(z_high.shape, BF16)] * 2),
+            pltpu.SemaphoreType.DMA((2 * x_local,)),
+            pltpu.SemaphoreType.DMA((3 + len(later),)),
+        ],
+    )(
+        *(
+            pltpu.with_memory_space_constraint(array, pltpu.HBM)
+            for array in (
+                to_tiles(inputs),
+                to_tiles(pre_act),
+                to_tiles(grad_out),
+                z_high,
+                z_low,
+                *later,
+            )
+        )
+    )
+    tx, ty, tyi, z_turned, mode_weight = later[:2], later[2:4], later[4:6], later[6:8], later[8]
     planes = exchange(chunks)
-    mode_rows = ky_local * 2 * hh_count
-    chunks, stats = call(
-        plane_kernel,
-        (struct((x_devices, y_devices, mode_rows, LANES)), struct((2, SUBLANES, LANES))),
+    local = call(
+        local_kernel,
+        struct((channels, x_local, SUBLANES, LANES)),
+        "local",
+        in_specs=held(3),
+        out_specs=held(1)[0],
+    )(point_weight, g_high, g_low)
+    mode_rows_count = ky_local * 2 * hh_count
+    chunks, stats, bias_grad = call(
+        functools.partial(plane_kernel, scale),
+        (
+            struct((x_devices, y_devices, mode_rows_count, LANES)),
+            struct((SUBLANES, LANES)),
+            struct((1, channels)),
+        ),
         "plane",
+        in_specs=held(5),
+        out_specs=held(3),
     )(planes, *tx, *ty)
-    modes = exchange(chunks.reshape(devices, mode_rows, LANES))
+    modes = exchange(chunks.reshape(devices, mode_rows_count, LANES))
+    modes = modes.reshape(devices * mode_rows_count, LANES)
+    chunks = call(
+        functools.partial(back_kernel, cells, channels),
+        struct((devices * SUBLANES, LANES)),
+        "back",
+        in_specs=held(2),
+        out_specs=held(1)[0],
+    )(modes, mode_weight)
+    back = exchange(chunks.reshape(devices, SUBLANES, LANES))
     block = (kx_local, 1, 2, kz_count, pairs)
-    block_spec = pl.BlockSpec(block, lambda k: (0, k, 0, 0, 0))
-    mode_grad, chunks = call(
-        lambda *refs: mode_kernel(cells, *refs),
-        (struct(mode_weight.shape), struct((devices * SUBLANES, LANES))),
-        "mode",
+    mode_grad = call(
+        functools.partial(outer_kernel, cells),
+        struct(mode_weight.shape),
+        "outer",
         grid=(ky_local,),
-        in_specs=[
-            whole((devices * mode_rows, LANES)),
-            whole(spread.shape),
-            whole(summed.shape),
-            block_spec,
-        ],
-        out_specs=(block_spec, whole((devices * SUBLANES, LANES))),
-    )(modes.reshape(devices * mode_rows, LANES), spread, summed, mode_weight)
-    back = exchange(chunks.reshape(devices, SUBLANES, LANES))
+        in_specs=held(2),
+        out_specs=pl.BlockSpec(block, lambda k: (0, k, 0, 0, 0)),
+    )(modes, spread)
     chunks = call(
-        inverse_kernel, struct((x_devices, y_devices, SUBLANES, LANES)), "inverse"
+        inverse_kernel,
+        struct((x_devices, y_devices, SUBLANES, LANES)),
+        "inverse",
+        in_specs=held(6),
+        out_specs=held(1)[0],
     )(back, stats, *tyi, *tx)
     near = exchange(chunks.reshape(devices, SUBLANES, LANES))
-    kron = (
-        point_weight[:, None, :, None] * jnp.eye(SUBLANES, dtype=F32)[None, :, None, :]
-    ).reshape(rows, rows)
     x_block = max(x_local // 4, 1)
-    g_spec = pl.BlockSpec((x_block, rows, LANES), lambda k: (k, 0, 0))
-    grad, point_grad, bias_grad = call(
-        lambda *refs: result_kernel(scale, *refs),
+    tile_spec = pl.BlockSpec((channels, x_block, SUBLANES, LANES), lambda k: (0, k, 0, 0))
+    grad, point_grad = call(
+        functools.partial(result_kernel, scale),
         (
             struct((channels, x_local, SUBLANES, LANES)),
             struct((channels, channels)),
-            struct((SUBLANES, channels)),
         ),
         "result",
         grid=(x_local // x_block,),
-        in_specs=[
-            whole((rows, LANES)),
-            whole((2, SUBLANES, LANES)),
-            whole((2 * LANES, LANES)),
-            whole((2 * LANES, LANES)),
-            whole((rows, rows)),
-            g_spec,
-            g_spec,
-        ],
-        out_specs=(
-            pl.BlockSpec((channels, x_block, SUBLANES, LANES), lambda k: (0, k, 0, 0)),
-            whole((channels, channels)),
-            whole((SUBLANES, channels)),
-        ),
-    )(near.reshape(rows, LANES), stats, z_high.T, z_low.T, kron, g_high, g_low)
+        in_specs=held(4),
+        out_specs=(tile_spec, pl.BlockSpec((channels, channels), lambda k: (0, 0))),
+        scratch_shapes=[pltpu.VMEM((rows, 6 * LANES), BF16)],
+    )(near.reshape(rows, LANES), *z_turned, local)
     return (from_tiles(grad, y_local, depth), point_grad, bias_grad[0], mode_grad)
 
 

time: 78.6 us -> 64.1 us (0.82)
  blocking collectives: 30.7 us -> 40.6 us
  local copies, waits for them, and re-layouts: 7.18 us -> 0.01 us
  waiting for transfers between devices: 9.05 us -> 2.62 us
  Pallas kernels: 22.4 us -> 17.4 us
  starting transfers between devices: 5.34 us -> 2.58 us
  other arithmetic: 2.55 us -> 0 us
    all_to_all x2 -> x3, blocking collectives: 30.7 us -> 40.6 us  [exchange(): return lax.all_to_all(chunks, axes, 0, 0)]
    all_to_all x2 -> x1, waiting for transfers between devices: 9.05 us -> 2.62 us  [exchange(): return lax.all_to_all(chunks, axes, 0, 0)]
    mul x1 -> x0, local copies, waits for them, and re-layouts: 4.7 us -> none  [transposed(): point_weight[:, None, :, None]]
    pallas_call x4 -> x6, Pallas kernels: 19.7 us -> 15.9 us  [the longest x1 4.47 us: transposed(): call(functools.partial(grid_kernel, len(later)), (struct((channels, 2, SU...]
    all_to_all x2 -> x1, starting transfers between devices: 5.34 us -> 2.58 us  [exchange(): return lax.all_to_all(chunks, axes, 0, 0)]
    mul x1 -> x0, other arithmetic: 2.55 us -> none  [transposed(): point_weight[:, None, :, None]]
    pallas_call x1, Pallas kernels: 2.78 us -> 1.45 us  [transposed(): call(inverse_kernel, struct((x_devices, y_devices, SUBLANES, LANES)), 'in...]
    unnamed x6 -> x4, local copies, waits for them, and re-layouts: 1.3 us -> 0.01 us
  transfers between devices with their start and end apart: 2 -> 1, of which waited for: 2 -> 1; matrix products, arithmetic and copies ran while one was open for 9% -> 0% of each run, Pallas kernels for 0% -> 9%
where the time goes in v1:
time: 64.1 us; the launch traced here: 63.9 us
  blocking collectives  40.6 us (63%)
  Pallas kernels  17.4 us (27%)
  waiting for transfers between devices  2.62 us (4%)
  starting transfers between devices  2.58 us (4%)
  between operations  0.68 us (1%)
    all_to_all x3, blocking collectives, exchange(): return lax.all_to_all(chunks, axes, 0, 0)  40.6 us
    pallas_call x1, Pallas kernels, transposed(): call(functools.partial(grid_kernel, len(later)), (struct((channels, 2, SU...  4.47 us
    pallas_call x1, Pallas kernels, transposed(): call(functools.partial(outer_kernel, cells), struct(mode_weight.shape), '...  3.69 us
    pallas_call x1, Pallas kernels, transposed(): call(functools.partial(result_kernel, scale), (struct((channels, x_local,...  2.92 us
    all_to_all x1, waiting for transfers between devices, exchange(): return lax.all_to_all(chunks, axes, 0, 0)  2.62 us
    all_to_all x1, starting transfers between devices, exchange(): return lax.all_to_all(chunks, axes, 0, 0)  2.58 us
    pallas_call x1, Pallas kernels, transposed(): call(functools.partial(back_kernel, cells, channels), struct((devices * S...  1.92 us
    pallas_call x1, Pallas kernels, transposed(): call(local_kernel, struct((channels, x_local, SUBLANES, LANES)), 'local',...  1.82 us
  transfers between devices with their start and end apart: 1, of which 1 were waited for; matrix products, arithmetic and copies ran while one was open for 0% of the time, Pallas kernels for 9%

profile of v1, /device:TPU:0, one launch (start us, length us, event | category | flops | bytes accessed | tf_op | source)
XLA Modules:
  0.0 63.9 jit_solution(12632767893525597349)
XLA Ops:
  0.6 4.5 %grid.1 = (f32[32,2,8,128]{3,2,1,0:T(8,128)S(1)}, bf16[8,256,128]{2,1,0:T(8,128)(2,1)S(1)}, bf16[8,256,128]{2,1,0:T(8,128)(2,1)S(1)}, bf16[512,512]{1,0:T(8,128)...) custom-call(bf16[32,8,8,128]{3,2,1,0:T(8,128)(2,1)} %bitcast.31, ...), custom_call_target="tpu_custom_call" | custom-call | tf_op jit(solution)/shard_map/grid/pallas_call | solution.py:662
  5.1 17.1 %all_to_all.20.r_ref = f32[32,2,8,128]{3,2,1,0:T(8,128)S(1)} all-to-all(f32[32,2,8,128]{3,2,1,0:T(8,128)S(1)} %get-tuple-element.21), channel_id=1, replica_groups=mesh['gx'=4,'gy'=8] {'gx','gy'}, dimensions={0} | all-to-all | bytes 524288 | tf_op jit(solution)/shard_map/all_to_all | solution.py:652
  22.2 0.0 copy-start.1
  22.3 1.1 %plane.1 = (f32[4,8,16,128]{3,2,1,0:T(8,128)S(1)}, f32[8,128]{1,0:T(8,128)S(1)}, f32[1,32]{1,0:T(1,128)}) custom-call(f32[32,2,8,128]{3,2,1,0:T(8,128)S(1)} %all_to_all.20.r_ref, bf16[512,512]{1,0:T(8,128)(2,1)S(1)} %get-tuple-element.22.txh_ref, bf16[512,512]{1,0:T(8,128)(2,1)S(1)} %get-tuple-element.23.txl_ref, ...), custom_call_target="tpu_custom_call" | custom-call | tf_op jit(solution)/shard_map/plane/pallas_call | solution.py:703
  23.3 12.7 %all_to_all.21 = f32[32,16,128]{2,1,0:T(8,128)S(1)} all-to-all(f32[32,16,128]{2,1,0:T(8,128)S(1)} %bitcast.30), channel_id=1, replica_groups=mesh['gx'=4,'gy'=8] {'gx','gy'}, dimensions={0} | all-to-all | bytes 524288 | tf_op jit(solution)/shard_map/all_to_all | solution.py:652
  36.0 0.0 copy-start
  36.0 1.9 %back.1 = f32[256,128]{1,0:T(8,128)S(1)} custom-call(f32[512,128]{1,0:T(8,128)S(1)} %bitcast.26, f32[8,4,2,16,1024]{4,3,2,1,0:T(8,128)S(1)} %get-tuple-element.27.weight_ref), custom_call_target="tpu_custom_call" | custom-call | tf_op jit(solution)/shard_map/back/pallas_call | solution.py:716
  37.9 10.8 %all_to_all.22.r_ref = f32[32,8,128]{2,1,0:T(8,128)S(1)} all-to-all(f32[32,8,128]{2,1,0:T(8,128)S(1)} %bitcast.29), channel_id=1, replica_groups=mesh['gx'=4,'gy'=8] {'gx','gy'}, dimensions={0} | all-to-all | bytes 262144 | tf_op jit(solution)/shard_map/all_to_all | solution.py:652
  48.8 1.4 %inverse.1 = f32[4,8,8,128]{3,2,1,0:T(8,128)} custom-call(f32[32,8,128]{2,1,0:T(8,128)S(1)} %all_to_all.22.r_ref, f32[8,128]{1,0:T(8,128)S(1)} %get-tuple-element.28.stat_ref, bf16[64,128]{1,0:T(8,128)(2,1)S(1)} %get-tuple-element.29.tyh_ref, bf16[64,128]{1,0:T(8,128)(2,1)S(1)} %get-tuple-element.30.tyl_ref, bf16[512,512]{1,0:T(8,128)(2,1)S(1)} %get-tuple-element.22.txh_ref, ...), custom_call_target="tpu_custom_call" | custom-call | tf_op jit(solution)/shard_map/inverse/pallas_call | solution.py:733
  50.2 2.6 %all-to-all-start.3 = ((f32[32,8,128]{2,1,0:T(8,128)}), f32[32,8,128]{2,1,0:T(8,128)S(1)}, u32[]{:S(2)}, u32[]{:S(2)}) async-start(f32[32,8,128]{2,1,0:T(8,128)} %bitcast.12), calls=%async_computation.3 | async-start | bytes 262144 | tf_op jit(solution)/shard_map/all_to_all | solution.py:652
  52.8 0.0 copy-done.1
  52.8 1.8 %local.1.local_ref = f32[32,8,8,128]{3,2,1,0:T(8,128)S(1)} custom-call(f32[32,32]{1,0:T(8,128)S(1)} %copy-done.1, bf16[8,256,128]{2,1,0:T(8,128)(2,1)S(1)} %get-tuple-element.33.ghi_ref, bf16[8,256,128]{2,1,0:T(8,128)(2,1)S(1)} %get-tuple-element.34.glo_ref), custom_call_target="tpu_custom_call" | custom-call | tf_op jit(solution)/shard_map/local/pallas_call | solution.py:695
  54.6 0.0 copy-done
  54.6 3.7 %outer.1 = f32[8,4,2,16,1024]{4,3,2,1,0:T(8,128)} custom-call(f32[512,128]{1,0:T(8,128)S(1)} %bitcast.27, bf16[128,1152]{1,0:T(8,128)(2,1)S(1)} %copy-done), custom_call_target="tpu_custom_call" | custom-call | tf_op jit(solution)/shard_map/outer/pallas_call | solution.py:725
  58.3 2.6 %all-to-all-done.3 = f32[32,8,128]{2,1,0:T(8,128)S(1)} async-done(((f32[32,8,128]{2,1,0:T(8,128)}), f32[32,8,128]{2,1,0:T(8,128)S(1)}, u32[]{:S(2)}, u32[]{:S(2)}) %all-to-all-start.3) | async-done | bytes 131104 | tf_op jit(solution)/shard_map/all_to_all | solution.py:652
  61.0 2.9 %result.1 = (f32[32,8,8,128]{3,2,1,0:T(8,128)}, f32[32,32]{1,0:T(8,128)}) custom-call(f32[256,128]{1,0:T(8,128)S(1)} %bitcast.28, bf16[256,128]{1,0:T(8,128)(2,1)S(1)} %get-tuple-element.31.hi_ref, bf16[256,128]{1,0:T(8,128)(2,1)S(1)} %get-tuple-element.32.lo_ref, f32[32,8,8,128]{3,2,1,0:T(8,128)S(1)} %local.1.local_ref), custom_call_target="tpu_custom_call" | custom-call | tf_op jit(solution)/shard_map/result/pallas_call | solution.py:743
Async XLA Ops:
  22.2 30.6 %copy-start.1 = (f32[32,32]{1,0:T(8,128)S(1)}, f32[32,32]{1,0:T(8,128)}, u32[]{:S(2)}) copy-start(f32[32,32]{1,0:T(8,128)} %weight_ref.1) | copy-start | bytes 12292
  36.0 18.6 %copy-start = (bf16[128,1152]{1,0:T(8,128)(2,1)S(1)}, bf16[128,1152]{1,0:T(8,128)(2,1)}, u32[]{:S(2)}) copy-start(bf16[128,1152]{1,0:T(8,128)(2,1)} %constant.32.clone.spread_ref) | copy-start | bytes 884740
  50.2 10.7 %all-to-all-start.3 = ((f32[32,8,128]{2,1,0:T(8,128)}), f32[32,8,128]{2,1,0:T(8,128)S(1)}, u32[]{:S(2)}, u32[]{:S(2)}) async-start(f32[32,8,128]{2,1,0:T(8,128)} %bitcast.12), calls=%async_computation.3 | async-start | bytes 262144 | tf_op jit(solution)/shard_map/all_to_all | solution.py:652

commit v2 on v1

--- a/solution.py
+++ b/solution.py
@@ -249,10 +249,14 @@
     return lax.dot_general(left, right, (((1,), (1,)), ((), ())), preferred_element_type=F32)
 
 
-def product(left, right, multiply=dot):
-    return (
-        multiply(left[0], right[0]) + multiply(left[0], right[1]) + multiply(left[1], right[0])
-    )
+def product(left, right):
+    left = jnp.concatenate([left[0], left[1], left[0]], axis=1)
+    return dot(left, jnp.concatenate([right[0], right[0], right[1]], axis=0))
+
+
+def product_rows(left, right):
+    left = jnp.concatenate([left[0], left[1], left[0]], axis=1)
+    return dot_rows(left, jnp.concatenate([right[0], right[0], right[1]], axis=1))
 
 
 def iota(shape, axis):
@@ -322,57 +326,77 @@
     return (iota(shape, 0) < y_local) & (iota(shape, 1) % (2 * HL) == HL)
 
 
+def only_x(table, x):
+    group = 2 * HL
+    zeros = jnp.zeros((LANES, table.shape[1]), table.dtype)
+    blocks = []
+    for start in range(0, table.shape[0], LANES):
+        at = start + x * group
+        blocks += [zeros[: x * group], table[at : at + group], zeros[(x + 1) * group :]]
+    return jnp.concatenate([block for block in blocks if block.shape[0] > 0], axis=0)
+
+
 def grid_kernel(count, *refs):
-    in_hbm, pre_hbm, out_grad_hbm, hi_hbm, lo_hbm = refs[:5]
-    later_hbm, refs = refs[5 : 5 + count], refs[5 + count :]
+    fields_hbm, refs = refs[:3], refs[3:]
+    later_hbm, refs = refs[:count], refs[count:]
     s_ref, ghi_ref, glo_ref = refs[:3]
     later, refs = refs[3 : 3 + count], refs[3 + count :]
-    in_ref, pre_ref, out_grad_ref, hi_ref, lo_ref, near_sems, far_sems = refs
+    in_ref, pre_ref, out_grad_ref, near_sems, far_sems = refs
+    hi_ref, lo_ref = later[:2]
     channels, x_local = in_ref.shape[:2]
     y_local = SUBLANES // 2
     rows = channels * SUBLANES
-    step = max(x_local // 4, 1)
-    parts = {}
-    for x in range(0, x_local, step):
-        at = (slice(None), pl.ds(x, step))
-        for index, pair in enumerate(((pre_hbm, pre_ref), (out_grad_hbm, out_grad_ref))):
-            sem = near_sems.at[2 * (x // step) + index]
-            parts[x, index] = pltpu.make_async_copy(pair[0].at[at], pair[1].at[at], sem)
-            parts[x, index].start()
-    whole_copies = [(in_hbm, in_ref), (hi_hbm, hi_ref), (lo_hbm, lo_ref)]
-    whole_copies = whole_copies + list(zip(later_hbm, later))
-    whole_copies = [
+    group = max(x_local // 4, 1)
+    parts = []
+    later_copies = [
         pltpu.make_async_copy(source, target, far_sems.at[index])
-        for index, (source, target) in enumerate(whole_copies)
+        for index, (source, target) in enumerate(zip(later_hbm, later))
     ]
-    for copy in whole_copies:
+    for x in range(0, x_local, group):
+        at = (slice(None), pl.ds(x, group))
+        copies = [
+            pltpu.make_async_copy(source.at[at], target.at[at], near_sems.at[index, x // group])
+            for index, (source, target) in enumerate(
+                zip(fields_hbm, (in_ref, pre_ref, out_grad_ref))
+            )
+        ]
+        parts.append(copies)
+        for copy in copies:
+            copy.start()
+        if x == 0:
+            for copy in later_copies[:2]:
+                copy.start()
+    for copy in later_copies[2:]:
         copy.start()
-    fields, highs, lows, tables_hi, tables_lo = [], [], [], [], []
-    for x in range(x_local):
-        if x % step == 0:
-            parts[x, 0].wait()
-            parts[x, 1].wait()
-        pre_grad = out_grad_ref[:, x].astype(F32) * gelu_slope(pre_ref[:, x])
-        high, low = split(pre_grad.reshape(rows, LANES))
-        ghi_ref[x] = high
-        glo_ref[x] = low
-        highs.append(high)
-        lows.append(low)
-    for copy in whole_copies[:3]:
-        copy.wait()
-    table_hi = hi_ref[...].astype(F32)
-    table_lo = lo_ref[...].astype(F32)
-    lane_x = iota(table_hi.shape, 1) % LANES // (2 * HL)
-    for x in range(x_local):
-        fields.append(in_ref[:, x].astype(F32).reshape(rows, LANES).astype(BF16))
-        tables_hi.append(jnp.where(lane_x == x, table_hi, 0.0).astype(BF16))
-        tables_lo.append(jnp.where(lane_x == x, table_lo, 0.0).astype(BF16))
-    field = jnp.concatenate(fields, axis=1)
-    high = jnp.concatenate(highs, axis=1)
-    low = jnp.concatenate(lows, axis=1)
-    table = (jnp.concatenate(tables_hi, axis=0), jnp.concatenate(tables_lo, axis=0))
-    raw_in = dot(field, table[0]) + dot(field, table[1])
-    raw_grad = product((high, low), table)
+    raw, gram = 0.0, 0.0
+    ones = jnp.ones((2 * SUBLANES, 2 * group * LANES), BF16)
+    for first in range(0, x_local, group):
+        for copy in parts[first // group]:
+            copy.wait()
+        fields, highs, lows = [], [], []
+        for x in range(first, first + group):
+            pre_grad = out_grad_ref[:, x].astype(F32) * gelu_slope(pre_ref[:, x])
+            high, low = split(pre_grad.reshape(rows, LANES))
+            ghi_ref[x] = high
+            glo_ref[x] = low
+            highs.append(high)
+            lows.append(low)
+            fields.append(in_ref[:, x].reshape(rows, LANES))
+        if first == 0:
+            for copy in later_copies[:2]:
+                copy.wait()
+        tables = [
+            only_x(ref[...], x) for ref in (hi_ref, lo_ref) for x in range(first, first + group)
+        ]
+        table = jnp.concatenate(tables, axis=1)
+        field = jnp.concatenate(fields * 2, axis=1)
+        high = jnp.concatenate(highs * 2, axis=1)
+        low = jnp.concatenate(lows * 2, axis=1)
+        raw += dot_rows(jnp.concatenate([field, high, low], axis=0), table)
+        both = jnp.concatenate(highs + lows, axis=1)
+        gram += dot_rows(jnp.concatenate([field, ones], axis=0), both)
+    raw_in, raw_grad = raw[:rows], raw[rows : 2 * rows] + raw[2 * rows :]
+    gram, bias = gram[:rows], gram[rows : rows + SUBLANES]
 
     tile = (channels, SUBLANES, LANES)
     sign = jnp.where(iota(tile, 2) % 2 == 0, 1.0, -1.0)
@@ -389,7 +413,6 @@
 
     wide = (channels, SUBLANES, rows)
     row, col = iota(wide, 1), iota(wide, 2)
-    gram = dot_rows(field, high) + dot_rows(field, low)
     trace = jnp.where(row == col % SUBLANES, gram.reshape(wide), 0.0)
     trace = jnp.sum(trace, axis=1, keepdims=True)
     at_row = row == col // SUBLANES // x_local
@@ -399,13 +422,11 @@
         iota(flat, 1) == iota(flat, 0) // SUBLANES % x_local * (2 * HL) + HL, 1.0, 0.0
     ).astype(BF16)
     weight_slots = dot(weight_rows[0], place) + dot(weight_rows[1], place)
-    ones = jnp.ones((2 * SUBLANES, field.shape[1]), BF16)
-    bias = (dot_rows(ones, high) + dot_rows(ones, low))[:SUBLANES]
     bias_rows = split(jnp.where(at_row[0], bias, 0.0))
     bias_slots = dot(bias_rows[0], place) + dot(bias_rows[1], place)
     s_ref[:, 0] = joined(raw_in) + weight_slots.reshape(tile)
     s_ref[:, 1] = joined(raw_grad) + bias_slots[None]
-    for copy in whole_copies[3:]:
+    for copy in later_copies[2:]:
         copy.wait()
 
 
@@ -419,19 +440,10 @@
     return jnp.dot(taken, place, precision=HIGHEST_PRECISION, preferred_element_type=F32)
 
 
-def plane_kernel(
-    scale, r_ref, txh_ref, txl_ref, tyh_ref, tyl_ref, s_ref, stat_ref, bias_ref
-):
+def plane_kernel(r_ref, txh_ref, txl_ref, tyh_ref, tyl_ref, s_ref, stat_ref):
     x_devices, y_devices = s_ref.shape[:2]
     y_local = SUBLANES // 2
-    stats = jnp.sum(r_ref[...], axis=0)
-    stat_ref[...] = stats[0]
-    channels = bias_ref.shape[1]
-    bias = jnp.zeros((SUBLANES, channels), F32)
-    for y in range(y_local):
-        row = jnp.where(iota((SUBLANES, LANES), 0) == y, stats[1], 0.0)
-        bias += from_slots(row, slot_place(channels, channels // y_local, y))
-    bias_ref[...] = jnp.sum(bias, axis=0, keepdims=True) * scale
+    stat_ref[...] = jnp.sum(r_ref[...], axis=0)
     values = jnp.where(slot_mask(y_local), 0.0, r_ref[...])
     values = values.reshape(x_devices, -1, LANES)
     wide = jnp.concatenate([values[g] for g in range(x_devices)], axis=1)
@@ -461,10 +473,11 @@
 def back_kernel(cells, channels, r_ref, weight_ref, s_ref):
     size = channels * channels
     kx_local, ky_local = weight_ref.shape[:2]
-    shape = (channels, size)
-    sums = jnp.where(iota(shape, 0) == iota(shape, 1) // channels, 1.0, 0.0).astype(BF16)
     count = kx_local * HL
-    times = size // LANES
+    width = SUBLANES * channels
+    shape = (2 * SUBLANES, 2 * width)
+    sums = iota(shape, 0) == iota(shape, 1) % width // channels
+    sums = jnp.where(sums, 1.0, 0.0).astype(BF16)
     group = LANES // channels // 2
     for start in range(0, ky_local, group):
         places = [(ky, hh) for ky in range(start, start + group) for hh in range(2)]
@@ -478,20 +491,23 @@
             while shift < LANES:
                 grad = grad + pltpu.roll(grad, shift, 1)
                 shift = shift * 2
-            grad_real, grad_imag = repeated(grad[:count], times), repeated(grad[count:], times)
+            grad_real = repeated(grad[:count], width // LANES)
+            grad_imag = repeated(grad[count:], width // LANES)
             rows = slice(hh * HL, (hh + 1) * HL)
-            mix_real = weight_ref[:, ky, 0, rows, :].reshape(count, size)
-            mix_imag = weight_ref[:, ky, 1, rows, :].reshape(count, size)
-            terms = jnp.concatenate(
-                [
-                    grad_real * mix_real + grad_imag * mix_imag,
-                    grad_imag * mix_real - grad_real * mix_imag,
-                ],
-                axis=0,
-            )
-            high, low = split(terms)
-            back = dot_rows(sums, high) + dot_rows(sums, low)
-            s_ref[pl.ds(ky * 2 + hh, channels, stride=SUBLANES), :] = back
+            for block in range(size // width):
+                at = slice(block * width, (block + 1) * width)
+                mix_real = weight_ref[:, ky, 0, rows, at].reshape(count, width)
+                mix_imag = weight_ref[:, ky, 1, rows, at].reshape(count, width)
+                terms = jnp.concatenate(
+                    [
+                        grad_real * mix_real + grad_imag * mix_imag,
+                        grad_imag * mix_real - grad_real * mix_imag,
+                    ],
+                    axis=0,
+                )
+                back = dot_rows(sums, jnp.concatenate(split(terms), axis=1))
+                at = block * SUBLANES * SUBLANES + ky * 2 + hh
+                s_ref[pl.ds(at, SUBLANES, stride=SUBLANES), :] = back[:SUBLANES]
 
 
 def outer_kernel(cells, r_ref, spread_ref, grad_ref):
@@ -529,9 +545,14 @@
         grad_ref[:, 0, 1, rows, :] = (in_real * grad_imag - in_imag * grad_real).reshape(tile)
 
 
-def local_kernel(weight_ref, ghi_ref, glo_ref, local_ref):
+def local_kernel(scale, weight_ref, ghi_ref, glo_ref, stat_ref, local_ref, bias_ref):
     channels, x_local = local_ref.shape[:2]
     rows = channels * SUBLANES
+    bias = jnp.zeros((SUBLANES, channels), F32)
+    for y in range(SUBLANES // 2):
+        row = jnp.where(iota((SUBLANES, LANES), 0) == y, stat_ref[1], 0.0)
+        bias += from_slots(row, slot_place(channels, x_local, y))
+    bias_ref[...] = jnp.sum(bias, axis=0, keepdims=True) * scale
     spread = jnp.where(
         iota((rows, channels), 0) // SUBLANES == iota((rows, channels), 1), 1.0, 0.0
     )
@@ -563,51 +584,52 @@
     turned = [sign * pltpu.roll(values[g], LANES // 2, 1) for g in range(x_devices)]
     both = jnp.concatenate([wide, jnp.concatenate(turned, axis=1)], axis=0)
     along_y = product((tyh_ref[...], tyl_ref[...]), split(both))
-    along_x = product(split(along_y), (txh_ref[...], txl_ref[...]), dot_rows)
+    along_x = product_rows(split(along_y), (txh_ref[...], txl_ref[...]))
     slots = slot_mask(y_local)
     for g in range(x_devices):
         block = along_x[:, g * LANES : (g + 1) * LANES].reshape(s_ref.shape[1:])
-        s_ref[g] = jnp.where(slots, stat_ref[...], block)
-
-
-def result_kernel(scale, r_ref, hi_ref, lo_ref, local_ref, grad_ref, point_ref, left_ref):
-    channels, x_block = grad_ref.shape[:2]
+        s_ref[g] = jnp.where(slots, stat_ref[0], block)
+
+
+def result_kernel(scale, r_ref, hi_ref, lo_ref, local_ref, grad_hbm, point_ref, grad_ref, sems):
+    channels, x_local = grad_ref.shape[:2]
     y_local = SUBLANES // 2
-    x_local = LANES // (2 * HL)
-    step = pl.program_id(0)
     rows = channels * SUBLANES
     tile = (channels, SUBLANES, LANES)
-
-    @pl.when(step == 0)
-    def _():
-        values = r_ref[...].reshape(tile)
-        turned = pltpu.roll(values, y_local, 1)
-        sign = jnp.where(iota(tile, 2) % 2 == 0, 1.0, -1.0)
-        upper = iota(tile, 1) < y_local
-        left = jnp.concatenate(
-            [
-                jnp.where(upper, values, sign * turned).reshape(rows, LANES),
-                jnp.where(upper, turned, sign * values).reshape(rows, LANES),
-            ],
-            axis=1,
-        )
-        high, low = split(left)
-        left_ref[...] = jnp.concatenate([high, low, high], axis=1)
-        point = jnp.zeros(point_ref.shape, F32)
-        for y in range(y_local):
-            taken = r_ref[pl.ds(y, channels, stride=SUBLANES), :]
-            point += from_slots(taken, slot_place(channels, x_local, y))
-        point_ref[...] = point * scale
-
-    table_hi = hi_ref[...].astype(F32)
-    table_lo = lo_ref[...].astype(F32)
-    row_x = iota(table_hi.shape, 0) % LANES // (2 * HL)
-    for k in range(x_block):
-        x = step * x_block + k
-        t_hi = jnp.where(row_x == x, table_hi, 0.0).astype(BF16)
-        t_lo = jnp.where(row_x == x, table_lo, 0.0).astype(BF16)
-        right = jnp.concatenate([t_hi, t_hi, t_lo], axis=0)
-        grad_ref[:, k] = dot(left_ref[...], right).reshape(tile) + local_ref[:, x]
+    values = r_ref[...].reshape(tile)
+    turned = pltpu.roll(values, y_local, 1)
+    sign = jnp.where(iota(tile, 2) % 2 == 0, 1.0, -1.0)
+    upper = iota(tile, 1) < y_local
+    left = jnp.concatenate(
+        [
+            jnp.where(upper, values, sign * turned).reshape(rows, LANES),
+            jnp.where(upper, turned, sign * values).reshape(rows, LANES),
+        ],
+        axis=1,
+    )
+    high, low = split(left)
+    left = jnp.concatenate([high, low, high], axis=1)
+    group = max(x_local // 4, 1)
+    copies = []
+    for first in range(0, x_local, group):
+        places = range(first, first + group)
+        t_hi = jnp.concatenate([only_x(hi_ref[...], x) for x in places], axis=1)
+        t_lo = jnp.concatenate([only_x(lo_ref[...], x) for x in places], axis=1)
+        block = dot(left, jnp.concatenate([t_hi, t_hi, t_lo], axis=0))
+        for x in places:
+            part = block[:, (x - first) * LANES : (x - first + 1) * LANES]
+            grad_ref[:, x] = part.reshape(tile) + local_ref[:, x]
+        at = (slice(None), pl.ds(first, group))
+        sem = sems.at[first // group]
+        copies.append(pltpu.make_async_copy(grad_ref.at[at], grad_hbm.at[at], sem))
+        copies[-1].start()
+    point = jnp.zeros(point_ref.shape, F32)
+    for y in range(y_local):
+        taken = r_ref[pl.ds(y, channels, stride=SUBLANES), :]
+        point += from_slots(taken, slot_place(channels, x_local, y))
+    point_ref[...] = point * scale
+    for copy in copies:
+        copy.wait()
 
 
 def call(kernel, out_shape, name, vmem=16, **options):
@@ -658,7 +680,7 @@
     spread = spread_table(channels)
 
     field_shape = (channels, x_local, SUBLANES, LANES)
-    later = (*tx, *ty, *tyi, z_high.T, z_low.T, mode_weight)
+    later = (z_high.T, z_low.T, *tx, *ty, *tyi, mode_weight)
     chunks, g_high, g_low, *later = call(
         functools.partial(grid_kernel, len(later)),
         (
@@ -669,13 +691,12 @@
         ),
         "grid",
         vmem=24,
-        in_specs=[pl.BlockSpec(memory_space=pltpu.HBM)] * (5 + len(later)),
+        in_specs=[pl.BlockSpec(memory_space=pltpu.HBM)] * (3 + len(later)),
         out_specs=held(3 + len(later)),
         scratch_shapes=[
             *([pltpu.VMEM(field_shape, BF16)] * 3),
-            *([pltpu.VMEM(z_high.shape, BF16)] * 2),
-            pltpu.SemaphoreType.DMA((2 * x_local,)),
-            pltpu.SemaphoreType.DMA((3 + len(later),)),
+            pltpu.SemaphoreType.DMA((3, x_local)),
+            pltpu.SemaphoreType.DMA((len(later),)),
         ],
     )(
         *(
@@ -684,33 +705,30 @@
                 to_tiles(inputs),
                 to_tiles(pre_act),
                 to_tiles(grad_out),
-                z_high,
-                z_low,
                 *later,
             )
         )
     )
-    tx, ty, tyi, z_turned, mode_weight = later[:2], later[2:4], later[4:6], later[6:8], later[8]
+    z_turned, tx, ty, tyi, mode_weight = later[:2], later[2:4], later[4:6], later[6:8], later[8]
     planes = exchange(chunks)
-    local = call(
-        local_kernel,
-        struct((channels, x_local, SUBLANES, LANES)),
-        "local",
-        in_specs=held(3),
-        out_specs=held(1)[0],
-    )(point_weight, g_high, g_low)
     mode_rows_count = ky_local * 2 * hh_count
-    chunks, stats, bias_grad = call(
-        functools.partial(plane_kernel, scale),
+    chunks, stats = call(
+        plane_kernel,
         (
             struct((x_devices, y_devices, mode_rows_count, LANES)),
-            struct((SUBLANES, LANES)),
-            struct((1, channels)),
+            struct((2, SUBLANES, LANES)),
         ),
         "plane",
         in_specs=held(5),
-        out_specs=held(3),
+        out_specs=held(2),
     )(planes, *tx, *ty)
+    local, bias_grad = call(
+        functools.partial(local_kernel, scale),
+        (struct(field_shape), struct((1, channels))),
+        "local",
+        in_specs=held(4),
+        out_specs=held(2),
+    )(point_weight, g_high, g_low, stats)
     modes = exchange(chunks.reshape(devices, mode_rows_count, LANES))
     modes = modes.reshape(devices * mode_rows_count, LANES)
     chunks = call(
@@ -738,19 +756,13 @@
         out_specs=held(1)[0],
     )(back, stats, *tyi, *tx)
     near = exchange(chunks.reshape(devices, SUBLANES, LANES))
-    x_block = max(x_local // 4, 1)
-    tile_spec = pl.BlockSpec((channels, x_block, SUBLANES, LANES), lambda k: (0, k, 0, 0))
     grad, point_grad = call(
         functools.partial(result_kernel, scale),
-        (
-            struct((channels, x_local, SUBLANES, LANES)),
-            struct((channels, channels)),
-        ),
+        (struct(field_shape), struct((channels, channels))),
         "result",
-        grid=(x_local // x_block,),
         in_specs=held(4),
-        out_specs=(tile_spec, pl.BlockSpec((channels, channels), lambda k: (0, 0))),
-        scratch_shapes=[pltpu.VMEM((rows, 6 * LANES), BF16)],
+        out_specs=(pl.BlockSpec(memory_space=pltpu.HBM), held(1)[0]),
+        scratch_shapes=[pltpu.VMEM(field_shape, F32), pltpu.SemaphoreType.DMA((x_local,))],
     )(near.reshape(rows, LANES), *z_turned, local)
     return (from_tiles(grad, y_local, depth), point_grad, bias_grad[0], mode_grad)
 

time: 64.1 us -> 61.7 us (0.963)
  Pallas kernels: 17.4 us -> 15.1 us
    pallas_call x1, Pallas kernels: 4.47 us -> 3.53 us  [transposed(): call(functools.partial(grid_kernel, len(later)), (struct((channels, 2, SU...]
    pallas_call x3, Pallas kernels: 5.82 us -> 4.93 us  [the longest x1 2.18 us: transposed(): call(functools.partial(result_kernel, scale), (struct(field_shape), struc...]
where the time goes in v2:
time: 61.7 us; the launch traced here: 61.4 us
  blocking collectives  40.7 us (66%)
  Pallas kernels  15.1 us (24%)
  starting transfers between devices  2.58 us (4%)
  waiting for transfers between devices  2.41 us (4%)
  between operations  0.69 us (1%)
    all_to_all x3, blocking collectives, exchange(): return lax.all_to_all(chunks, axes, 0, 0)  40.7 us
    pallas_call x1, Pallas kernels, transposed(): call(functools.partial(outer_kernel, cells), struct(mode_weight.shape), '...  3.69 us
    pallas_call x1, Pallas kernels, transposed(): call(functools.partial(grid_kernel, len(later)), (struct((channels, 2, SU...  3.53 us
    all_to_all x1, starting transfers between devices, exchange(): return lax.all_to_all(chunks, axes, 0, 0)  2.58 us
    all_to_all x1, waiting for transfers between devices, exchange(): return lax.all_to_all(chunks, axes, 0, 0)  2.41 us
    pallas_call x1, Pallas kernels, transposed(): call(functools.partial(result_kernel, scale), (struct(field_shape), struc...  2.18 us
    pallas_call x1, Pallas kernels, transposed(): call(functools.partial(local_kernel, scale), (struct(field_shape), struct...  2.03 us
    pallas_call x1, Pallas kernels, transposed(): call(functools.partial(back_kernel, cells, channels), struct((devices * S...  1.48 us
  transfers between devices with their start and end apart: 1, of which 1 were waited for; matrix products, arithmetic and copies ran while one was open for 0% of the time, Pallas kernels for 9%

profile of v2, /device:TPU:0, one launch (start us, length us, event | category | flops | bytes accessed | tf_op | source)
XLA Modules:
  0.0 61.4 jit_solution(903054045436100896)
XLA Ops:
  0.6 3.5 %grid.1 = (f32[32,2,8,128]{3,2,1,0:T(8,128)S(1)}, bf16[8,256,128]{2,1,0:T(8,128)(2,1)S(1)}, bf16[8,256,128]{2,1,0:T(8,128)(2,1)S(1)}, bf16[256,128]{1,0:T(8,128)...) custom-call(bf16[32,8,8,128]{3,2,1,0:T(8,128)(2,1)} %bitcast.31, ...), custom_call_target="tpu_custom_call" | custom-call | tf_op jit(solution)/shard_map/grid/pallas_call | solution.py:684
  4.2 17.1 %all_to_all.20.r_ref = f32[32,2,8,128]{3,2,1,0:T(8,128)S(1)} all-to-all(f32[32,2,8,128]{3,2,1,0:T(8,128)S(1)} %get-tuple-element.22), channel_id=1, replica_groups=mesh['gx'=4,'gy'=8] {'gx','gy'}, dimensions={0} | all-to-all | bytes 524288 | tf_op jit(solution)/shard_map/all_to_all | solution.py:674
  21.3 0.0 copy-start.1
  21.3 0.7 %plane.1 = (f32[4,8,16,128]{3,2,1,0:T(8,128)S(1)}, f32[2,8,128]{2,1,0:T(8,128)S(1)}) custom-call(f32[32,2,8,128]{3,2,1,0:T(8,128)S(1)} %all_to_all.20.r_ref, bf16[512,512]{1,0:T(8,128)(2,1)S(1)} %get-tuple-element.23.txh_ref, bf16[512,512]{1,0:T(8,128)(2,1)S(1)} %get-tuple-element.24.txl_ref, bf16[128,256]{1,0:T(8,128)(2,1)S(1)} %get-tuple-element.25.tyh_ref, ...), custom_call_target="tpu_custom_call" | custom-call | tf_op jit(solution)/shard_map/plane/pallas_call | solution.py:715
  22.0 0.0 copy-start
  22.0 12.7 %all_to_all.21 = f32[32,16,128]{2,1,0:T(8,128)S(1)} all-to-all(f32[32,16,128]{2,1,0:T(8,128)S(1)} %bitcast.30), channel_id=1, replica_groups=mesh['gx'=4,'gy'=8] {'gx','gy'}, dimensions={0} | all-to-all | bytes 524288 | tf_op jit(solution)/shard_map/all_to_all | solution.py:674
  34.7 1.5 %back.1 = f32[256,128]{1,0:T(8,128)S(1)} custom-call(f32[512,128]{1,0:T(8,128)S(1)} %bitcast.26, f32[8,4,2,16,1024]{4,3,2,1,0:T(8,128)S(1)} %get-tuple-element.28.weight_ref), custom_call_target="tpu_custom_call" | custom-call | tf_op jit(solution)/shard_map/back/pallas_call | solution.py:734
  36.2 10.8 %all_to_all.22.r_ref = f32[32,8,128]{2,1,0:T(8,128)S(1)} all-to-all(f32[32,8,128]{2,1,0:T(8,128)S(1)} %bitcast.29), channel_id=1, replica_groups=mesh['gx'=4,'gy'=8] {'gx','gy'}, dimensions={0} | all-to-all | bytes 262144 | tf_op jit(solution)/shard_map/all_to_all | solution.py:674
  47.0 1.4 %inverse.1 = f32[4,8,8,128]{3,2,1,0:T(8,128)} custom-call(f32[32,8,128]{2,1,0:T(8,128)S(1)} %all_to_all.22.r_ref, f32[2,8,128]{2,1,0:T(8,128)S(1)} %get-tuple-element.29.stat_ref, bf16[64,128]{1,0:T(8,128)(2,1)S(1)} %get-tuple-element.30.tyh_ref, bf16[64,128]{1,0:T(8,128)(2,1)S(1)} %get-tuple-element.31.tyl_ref, ...), custom_call_target="tpu_custom_call" | custom-call | tf_op jit(solution)/shard_map/inverse/pallas_call | solution.py:751
  48.5 2.6 %all-to-all-start.3 = ((f32[32,8,128]{2,1,0:T(8,128)}), f32[32,8,128]{2,1,0:T(8,128)S(1)}, u32[]{:S(2)}, u32[]{:S(2)}) async-start(f32[32,8,128]{2,1,0:T(8,128)} %bitcast.12), calls=%async_computation.3 | async-start | bytes 262144 | tf_op jit(solution)/shard_map/all_to_all | solution.py:674
  51.1 0.0 copy-done.1
  51.1 2.0 %local.1 = (f32[32,8,8,128]{3,2,1,0:T(8,128)S(1)}, f32[1,32]{1,0:T(1,128)}) custom-call(f32[32,32]{1,0:T(8,128)S(1)} %copy-done.1, bf16[8,256,128]{2,1,0:T(8,128)(2,1)S(1)} %get-tuple-element.34.ghi_ref, bf16[8,256,128]{2,1,0:T(8,128)(2,1)S(1)} %get-tuple-element.35.glo_ref, f32[2,8,128]{2,1,0:T(8,128)S(1)} %get-tuple-element.29.stat_ref), custom_call_target="tpu_custom_call" | custom-call | tf_op jit(solution)/shard_map/local/pallas_call | solution.py:725
  53.1 0.0 copy-done
  53.1 3.7 %outer.1 = f32[8,4,2,16,1024]{4,3,2,1,0:T(8,128)} custom-call(f32[512,128]{1,0:T(8,128)S(1)} %bitcast.27, bf16[128,1152]{1,0:T(8,128)(2,1)S(1)} %copy-done), custom_call_target="tpu_custom_call" | custom-call | tf_op jit(solution)/shard_map/outer/pallas_call | solution.py:743
  56.8 2.4 %all-to-all-done.3 = f32[32,8,128]{2,1,0:T(8,128)S(1)} async-done(((f32[32,8,128]{2,1,0:T(8,128)}), f32[32,8,128]{2,1,0:T(8,128)S(1)}, u32[]{:S(2)}, u32[]{:S(2)}) %all-to-all-start.3) | async-done | bytes 131104 | tf_op jit(solution)/shard_map/all_to_all | solution.py:674
  59.2 2.2 %result.1 = (f32[32,8,8,128]{3,2,1,0:T(8,128)}, f32[32,32]{1,0:T(8,128)}) custom-call(f32[256,128]{1,0:T(8,128)S(1)} %bitcast.28, bf16[256,128]{1,0:T(8,128)(2,1)S(1)} %get-tuple-element.32.hi_ref, bf16[256,128]{1,0:T(8,128)(2,1)S(1)} %get-tuple-element.33.lo_ref, f32[32,8,8,128]{3,2,1,0:T(8,128)S(1)} %get-tuple-element.36.local_ref), custom_call_target="tpu_custom_call" | custom-call | tf_op jit(solution)/shard_map/result/pallas_call | solution.py:759
Async XLA Ops:
  21.3 29.8 %copy-start.1 = (f32[32,32]{1,0:T(8,128)S(1)}, f32[32,32]{1,0:T(8,128)}, u32[]{:S(2)}) copy-start(f32[32,32]{1,0:T(8,128)} %weight_ref.1) | copy-start | bytes 12292
  22.0 31.1 %copy-start = (bf16[128,1152]{1,0:T(8,128)(2,1)S(1)}, bf16[128,1152]{1,0:T(8,128)(2,1)}, u32[]{:S(2)}) copy-start(bf16[128,1152]{1,0:T(8,128)(2,1)} %constant.26.clone.spread_ref) | copy-start | bytes 884740
  48.5 10.7 %all-to-all-start.3 = ((f32[32,8,128]{2,1,0:T(8,128)}), f32[32,8,128]{2,1,0:T(8,128)S(1)}, u32[]{:S(2)}, u32[]{:S(2)}) async-start(f32[32,8,128]{2,1,0:T(8,128)} %bitcast.12), calls=%async_computation.3 | async-start | bytes 262144 | tf_op jit(solution)/shard_map/all_to_all | solution.py:674

commit v3 on v2

--- a/solution.py
+++ b/solution.py
@@ -437,7 +437,12 @@
 
 
 def from_slots(taken, place):
-    return jnp.dot(taken, place, precision=HIGHEST_PRECISION, preferred_element_type=F32)
+    high = taken.astype(BF16)
+    middle, low = split(taken - high.astype(F32))
+    place = place.astype(BF16)
+    return dot(
+        jnp.concatenate([high, middle, low], axis=1), jnp.concatenate([place] * 3, axis=0)
+    )
 
 
 def plane_kernel(r_ref, txh_ref, txl_ref, tyh_ref, tyl_ref, s_ref, stat_ref):
@@ -600,28 +605,44 @@
     turned = pltpu.roll(values, y_local, 1)
     sign = jnp.where(iota(tile, 2) % 2 == 0, 1.0, -1.0)
     upper = iota(tile, 1) < y_local
-    left = jnp.concatenate(
-        [
-            jnp.where(upper, values, sign * turned).reshape(rows, LANES),
-            jnp.where(upper, turned, sign * values).reshape(rows, LANES),
-        ],
-        axis=1,
-    )
-    high, low = split(left)
-    left = jnp.concatenate([high, low, high], axis=1)
-    group = max(x_local // 4, 1)
+    halves = [
+        jnp.where(upper, values, sign * turned).reshape(rows, LANES),
+        jnp.where(upper, turned, sign * values).reshape(rows, LANES),
+    ]
+    highs = [half.astype(BF16).astype(F32) for half in halves]
+    parts = [*highs, *(half - high for half, high in zip(halves, highs))]
+    count = len(parts)
+    width = LANES // count
+    places = width // (2 * HL)
+    parts = [part if k == 0 else pltpu.roll(part, k * width, 1) for k, part in enumerate(parts)]
+    lane = iota((rows, LANES), 1) // width
+    group = 2 * HL
+    zeros = jnp.zeros((group, LANES), BF16)
+
+    def rows_of(ref, part, first):
+        blocks = []
+        for k in range(places):
+            at = part % 2 * LANES + (first + k) * group
+            row = [zeros] * places
+            row[k] = ref[at : at + group, :]
+            blocks.append(jnp.concatenate(row, axis=1))
+        return jnp.concatenate(blocks, axis=0)
+
     copies = []
-    for first in range(0, x_local, group):
-        places = range(first, first + group)
-        t_hi = jnp.concatenate([only_x(hi_ref[...], x) for x in places], axis=1)
-        t_lo = jnp.concatenate([only_x(lo_ref[...], x) for x in places], axis=1)
-        block = dot(left, jnp.concatenate([t_hi, t_hi, t_lo], axis=0))
-        for x in places:
-            part = block[:, (x - first) * LANES : (x - first + 1) * LANES]
-            grad_ref[:, x] = part.reshape(tile) + local_ref[:, x]
-        at = (slice(None), pl.ds(first, group))
-        sem = sems.at[first // group]
-        copies.append(pltpu.make_async_copy(grad_ref.at[at], grad_hbm.at[at], sem))
+    for index in range(x_local // places):
+        first = index * places
+        left = parts[0]
+        for k in range(1, count):
+            left = jnp.where(lane == (index + k) % count, parts[k], left)
+        left = left.astype(BF16)
+        order = [(k - index) % count for k in range(count)]
+        right = [rows_of(ref, part, first) for ref in (hi_ref, lo_ref) for part in order]
+        block = dot(jnp.concatenate([left, left], axis=1), jnp.concatenate(right, axis=0))
+        for k in range(places):
+            part = block[:, k * LANES : (k + 1) * LANES]
+            grad_ref[:, first + k] = part.reshape(tile) + local_ref[:, first + k]
+        at = (slice(None), pl.ds(first, places))
+        copies.append(pltpu.make_async_copy(grad_ref.at[at], grad_hbm.at[at], sems.at[index]))
         copies[-1].start()
     point = jnp.zeros(point_ref.shape, F32)
     for y in range(y_local):

time: 61.7 us -> 61.4 us (level)
  no operation moved by 1% of the time
where the time goes in v3:
time: 61.4 us; the launch traced here: 61.2 us
  blocking collectives  40.7 us (66%)
  Pallas kernels  14.7 us (24%)
  starting transfers between devices  2.58 us (4%)
  waiting for transfers between devices  2.55 us (4%)
  between operations  0.69 us (1%)
    all_to_all x3, blocking collectives, exchange(): return lax.all_to_all(chunks, axes, 0, 0)  40.7 us
    pallas_call x1, Pallas kernels, transposed(): call(functools.partial(outer_kernel, cells), struct(mode_weight.shape), '...  3.69 us
    pallas_call x1, Pallas kernels, transposed(): call(functools.partial(grid_kernel, len(later)), (struct((channels, 2, SU...  3.53 us
    all_to_all x1, starting transfers between devices, exchange(): return lax.all_to_all(chunks, axes, 0, 0)  2.58 us
    all_to_all x1, waiting for transfers between devices, exchange(): return lax.all_to_all(chunks, axes, 0, 0)  2.55 us
    pallas_call x1, Pallas kernels, transposed(): call(functools.partial(result_kernel, scale), (struct(field_shape), struc...  1.94 us
    pallas_call x1, Pallas kernels, transposed(): call(functools.partial(local_kernel, scale), (struct(field_shape), struct...  1.89 us
    pallas_call x1, Pallas kernels, transposed(): call(functools.partial(back_kernel, cells, channels), struct((devices * S...  1.48 us
  transfers between devices with their start and end apart: 1, of which 1 were waited for; matrix products, arithmetic and copies ran while one was open for 0% of the time, Pallas kernels for 9%

profile of v3, /device:TPU:0, one launch (start us, length us, event | category | flops | bytes accessed | tf_op | source)
XLA Modules:
  0.0 61.2 jit_solution(4977569744001276530)
XLA Ops:
  0.6 3.5 %grid.1 = (f32[32,2,8,128]{3,2,1,0:T(8,128)S(1)}, bf16[8,256,128]{2,1,0:T(8,128)(2,1)S(1)}, bf16[8,256,128]{2,1,0:T(8,128)(2,1)S(1)}, bf16[256,128]{1,0:T(8,128)...) custom-call(bf16[32,8,8,128]{3,2,1,0:T(8,128)(2,1)} %bitcast.31, ...), custom_call_target="tpu_custom_call" | custom-call | tf_op jit(solution)/shard_map/grid/pallas_call | solution.py:705
  4.2 17.1 %all_to_all.20.r_ref = f32[32,2,8,128]{3,2,1,0:T(8,128)S(1)} all-to-all(f32[32,2,8,128]{3,2,1,0:T(8,128)S(1)} %get-tuple-element.22), channel_id=1, replica_groups=mesh['gx'=4,'gy'=8] {'gx','gy'}, dimensions={0} | all-to-all | bytes 524288 | tf_op jit(solution)/shard_map/all_to_all | solution.py:695
  21.3 0.0 copy-start.1
  21.3 0.7 %plane.1 = (f32[4,8,16,128]{3,2,1,0:T(8,128)S(1)}, f32[2,8,128]{2,1,0:T(8,128)S(1)}) custom-call(f32[32,2,8,128]{3,2,1,0:T(8,128)S(1)} %all_to_all.20.r_ref, bf16[512,512]{1,0:T(8,128)(2,1)S(1)} %get-tuple-element.23.txh_ref, bf16[512,512]{1,0:T(8,128)(2,1)S(1)} %get-tuple-element.24.txl_ref, bf16[128,256]{1,0:T(8,128)(2,1)S(1)} %get-tuple-element.25.tyh_ref, ...), custom_call_target="tpu_custom_call" | custom-call | tf_op jit(solution)/shard_map/plane/pallas_call | solution.py:736
  22.0 0.0 copy-start
  22.0 12.7 %all_to_all.21 = f32[32,16,128]{2,1,0:T(8,128)S(1)} all-to-all(f32[32,16,128]{2,1,0:T(8,128)S(1)} %bitcast.30), channel_id=1, replica_groups=mesh['gx'=4,'gy'=8] {'gx','gy'}, dimensions={0} | all-to-all | bytes 524288 | tf_op jit(solution)/shard_map/all_to_all | solution.py:695
  34.7 1.5 %back.1 = f32[256,128]{1,0:T(8,128)S(1)} custom-call(f32[512,128]{1,0:T(8,128)S(1)} %bitcast.26, f32[8,4,2,16,1024]{4,3,2,1,0:T(8,128)S(1)} %get-tuple-element.28.weight_ref), custom_call_target="tpu_custom_call" | custom-call | tf_op jit(solution)/shard_map/back/pallas_call | solution.py:755
  36.2 10.8 %all_to_all.22.r_ref = f32[32,8,128]{2,1,0:T(8,128)S(1)} all-to-all(f32[32,8,128]{2,1,0:T(8,128)S(1)} %bitcast.29), channel_id=1, replica_groups=mesh['gx'=4,'gy'=8] {'gx','gy'}, dimensions={0} | all-to-all | bytes 262144 | tf_op jit(solution)/shard_map/all_to_all | solution.py:695
  47.0 1.4 %inverse.1 = f32[4,8,8,128]{3,2,1,0:T(8,128)} custom-call(f32[32,8,128]{2,1,0:T(8,128)S(1)} %all_to_all.22.r_ref, f32[2,8,128]{2,1,0:T(8,128)S(1)} %get-tuple-element.29.stat_ref, bf16[64,128]{1,0:T(8,128)(2,1)S(1)} %get-tuple-element.30.tyh_ref, bf16[64,128]{1,0:T(8,128)(2,1)S(1)} %get-tuple-element.31.tyl_ref, ...), custom_call_target="tpu_custom_call" | custom-call | tf_op jit(solution)/shard_map/inverse/pallas_call | solution.py:772
  48.5 2.6 %all-to-all-start.3 = ((f32[32,8,128]{2,1,0:T(8,128)}), f32[32,8,128]{2,1,0:T(8,128)S(1)}, u32[]{:S(2)}, u32[]{:S(2)}) async-start(f32[32,8,128]{2,1,0:T(8,128)} %bitcast.12), calls=%async_computation.3 | async-start | bytes 262144 | tf_op jit(solution)/shard_map/all_to_all | solution.py:695
  51.1 0.0 copy-done.1
  51.1 1.9 %local.1 = (f32[32,8,8,128]{3,2,1,0:T(8,128)S(1)}, f32[1,32]{1,0:T(1,128)}) custom-call(f32[32,32]{1,0:T(8,128)S(1)} %copy-done.1, bf16[8,256,128]{2,1,0:T(8,128)(2,1)S(1)} %get-tuple-element.34.ghi_ref, bf16[8,256,128]{2,1,0:T(8,128)(2,1)S(1)} %get-tuple-element.35.glo_ref, f32[2,8,128]{2,1,0:T(8,128)S(1)} %get-tuple-element.29.stat_ref), custom_call_target="tpu_custom_call" | custom-call | tf_op jit(solution)/shard_map/local/pallas_call | solution.py:746
  53.0 0.0 copy-done
  53.0 3.7 %outer.1 = f32[8,4,2,16,1024]{4,3,2,1,0:T(8,128)} custom-call(f32[512,128]{1,0:T(8,128)S(1)} %bitcast.27, bf16[128,1152]{1,0:T(8,128)(2,1)S(1)} %copy-done), custom_call_target="tpu_custom_call" | custom-call | tf_op jit(solution)/shard_map/outer/pallas_call | solution.py:764
  56.7 2.5 %all-to-all-done.3 = f32[32,8,128]{2,1,0:T(8,128)S(1)} async-done(((f32[32,8,128]{2,1,0:T(8,128)}), f32[32,8,128]{2,1,0:T(8,128)S(1)}, u32[]{:S(2)}, u32[]{:S(2)}) %all-to-all-start.3) | async-done | bytes 131104 | tf_op jit(solution)/shard_map/all_to_all | solution.py:695
  59.2 1.9 %result.1 = (f32[32,8,8,128]{3,2,1,0:T(8,128)}, f32[32,32]{1,0:T(8,128)}) custom-call(f32[256,128]{1,0:T(8,128)S(1)} %bitcast.28, bf16[256,128]{1,0:T(8,128)(2,1)S(1)} %get-tuple-element.32.hi_ref, bf16[256,128]{1,0:T(8,128)(2,1)S(1)} %get-tuple-element.33.lo_ref, f32[32,8,8,128]{3,2,1,0:T(8,128)S(1)} %get-tuple-element.36.local_ref), custom_call_target="tpu_custom_call" | custom-call | tf_op jit(solution)/shard_map/result/pallas_call | solution.py:780
Async XLA Ops:
  21.3 29.8 %copy-start.1 = (f32[32,32]{1,0:T(8,128)S(1)}, f32[32,32]{1,0:T(8,128)}, u32[]{:S(2)}) copy-start(f32[32,32]{1,0:T(8,128)} %weight_ref.1) | copy-start | bytes 12292
  22.0 30.9 %copy-start = (bf16[128,1152]{1,0:T(8,128)(2,1)S(1)}, bf16[128,1152]{1,0:T(8,128)(2,1)}, u32[]{:S(2)}) copy-start(bf16[128,1152]{1,0:T(8,128)(2,1)} %constant.26.clone.spread_ref) | copy-start | bytes 884740
  48.5 10.7 %all-to-all-start.3 = ((f32[32,8,128]{2,1,0:T(8,128)}), f32[32,8,128]{2,1,0:T(8,128)S(1)}, u32[]{:S(2)}, u32[]{:S(2)}) async-start(f32[32,8,128]{2,1,0:T(8,128)} %bitcast.12), calls=%async_computation.3 | async-start | bytes 262144 | tf_op jit(solution)/shard_map/all_to_all | solution.py:695

commit v4 on v3

--- a/solution.py
+++ b/solution.py
@@ -445,13 +445,33 @@
     )
 
 
-def plane_kernel(r_ref, txh_ref, txl_ref, tyh_ref, tyl_ref, s_ref, stat_ref):
-    x_devices, y_devices = s_ref.shape[:2]
+def exchange_order(x_devices, y_devices):
+    along = list(range(y_devices))
+    middle = y_devices // 4 * 2
+    along[:2], along[middle : middle + 2] = along[middle : middle + 2], along[:2]
+    return [g * y_devices + k for g in range(x_devices) for k in along]
+
+
+def by_device(order, x_devices):
+    place = sorted(range(len(order)), key=order.__getitem__)
+    y_devices = len(order) // x_devices
+    return [place[g * y_devices : (g + 1) * y_devices] for g in range(x_devices)]
+
+
+def plane_kernel(places, r_ref, txh_ref, txl_ref, tyh_ref, tyl_ref, s_ref, stat_ref):
     y_local = SUBLANES // 2
+    x_devices = len(places)
     stat_ref[...] = jnp.sum(r_ref[...], axis=0)
-    values = jnp.where(slot_mask(y_local), 0.0, r_ref[...])
-    values = values.reshape(x_devices, -1, LANES)
-    wide = jnp.concatenate([values[g] for g in range(x_devices)], axis=1)
+    slots = slot_mask(y_local)
+    wide = jnp.concatenate(
+        [
+            jnp.concatenate(
+                [jnp.where(slots, 0.0, r_ref[p]).reshape(-1, LANES) for p in row], axis=0
+            )
+            for row in places
+        ],
+        axis=1,
+    )
     along_x = product(split(wide), (txh_ref[...], txl_ref[...]))
     lane = iota((along_x.shape[0], LANES), 1)
     sign = jnp.where(lane < LANES // 2, 1.0, -1.0)
@@ -461,8 +481,10 @@
     ]
     both = jnp.concatenate([along_x, jnp.concatenate(turned, axis=1)], axis=0)
     along_y = product((tyh_ref[...], tyl_ref[...]), split(both))
-    for g in range(x_devices):
-        s_ref[g] = along_y[:, g * LANES : (g + 1) * LANES].reshape(s_ref.shape[1:])
+    count = s_ref.shape[1]
+    for g, row in enumerate(places):
+        for k, p in enumerate(row):
+            s_ref[p] = along_y[k * count : (k + 1) * count, g * LANES : (g + 1) * LANES]
 
 
 def mode_rows(r_ref, picks, channels):
@@ -579,21 +601,21 @@
         local_ref[:, x] = dot(left, right).reshape(channels, SUBLANES, LANES)
 
 
-def inverse_kernel(r_ref, stat_ref, tyh_ref, tyl_ref, txh_ref, txl_ref, s_ref):
-    x_devices, y_devices = s_ref.shape[:2]
+def inverse_kernel(places, r_ref, stat_ref, tyh_ref, tyl_ref, txh_ref, txl_ref, s_ref):
     y_local = SUBLANES // 2
-    values = r_ref[...].reshape(x_devices, y_devices * SUBLANES, LANES)
-    lane = iota(values.shape[1:], 1)
+    values = [jnp.concatenate([r_ref[p] for p in row], axis=0) for row in places]
+    lane = iota(values[0].shape, 1)
     sign = jnp.where(lane < LANES // 2, -1.0, 1.0)
-    wide = jnp.concatenate([values[g] for g in range(x_devices)], axis=1)
-    turned = [sign * pltpu.roll(values[g], LANES // 2, 1) for g in range(x_devices)]
+    wide = jnp.concatenate(values, axis=1)
+    turned = [sign * pltpu.roll(value, LANES // 2, 1) for value in values]
     both = jnp.concatenate([wide, jnp.concatenate(turned, axis=1)], axis=0)
     along_y = product((tyh_ref[...], tyl_ref[...]), split(both))
     along_x = product_rows(split(along_y), (txh_ref[...], txl_ref[...]))
     slots = slot_mask(y_local)
-    for g in range(x_devices):
-        block = along_x[:, g * LANES : (g + 1) * LANES].reshape(s_ref.shape[1:])
-        s_ref[g] = jnp.where(slots, stat_ref[0], block)
+    for g, row in enumerate(places):
+        for k, p in enumerate(row):
+            block = along_x[k * SUBLANES : (k + 1) * SUBLANES, g * LANES : (g + 1) * LANES]
+            s_ref[p] = jnp.where(slots, stat_ref[0], block)
 
 
 def result_kernel(scale, r_ref, hi_ref, lo_ref, local_ref, grad_hbm, point_ref, grad_ref, sems):
@@ -686,13 +708,15 @@
     cells = x_local * x_devices * y_local * y_devices * depth
     scale = 1.0 / math.sqrt(cells)
     axes = ("gx", "gy")
+    order = exchange_order(x_devices, y_devices)
+    places = by_device(order, x_devices)
     rows = channels * SUBLANES
 
     def struct(shape, kind=F32):
         return jax.ShapeDtypeStruct(shape, kind)
 
     def exchange(chunks):
-        return lax.all_to_all(chunks, axes, 0, 0)
+        return lax.all_to_all(chunks, axes, 0, 0, axis_index_groups=[order])
 
     z_high, z_low = split_table(depth_table(depth, kz_count, x_local))
     tx = split_table(x_table(x_devices, x_local, kx_local))
@@ -734,9 +758,9 @@
     planes = exchange(chunks)
     mode_rows_count = ky_local * 2 * hh_count
     chunks, stats = call(
-        plane_kernel,
+        functools.partial(plane_kernel, places),
         (
-            struct((x_devices, y_devices, mode_rows_count, LANES)),
+            struct((devices, mode_rows_count, LANES)),
             struct((2, SUBLANES, LANES)),
         ),
         "plane",
@@ -750,7 +774,7 @@
         in_specs=held(4),
         out_specs=held(2),
     )(point_weight, g_high, g_low, stats)
-    modes = exchange(chunks.reshape(devices, mode_rows_count, LANES))
+    modes = exchange(chunks)
     modes = modes.reshape(devices * mode_rows_count, LANES)
     chunks = call(
         functools.partial(back_kernel, cells, channels),
@@ -770,13 +794,13 @@
         out_specs=pl.BlockSpec(block, lambda k: (0, k, 0, 0, 0)),
     )(modes, spread)
     chunks = call(
-        inverse_kernel,
-        struct((x_devices, y_devices, SUBLANES, LANES)),
+        functools.partial(inverse_kernel, places),
+        struct((devices, SUBLANES, LANES)),
         "inverse",
         in_specs=held(6),
         out_specs=held(1)[0],
     )(back, stats, *tyi, *tx)
-    near = exchange(chunks.reshape(devices, SUBLANES, LANES))
+    near = exchange(chunks)
     grad, point_grad = call(
         functools.partial(result_kernel, scale),
         (struct(field_shape), struct((channels, channels))),

time: 61.4 us -> 60 us (0.977)
  blocking collectives: 40.7 us -> 39.8 us
    all_to_all x3, blocking collectives: 40.7 us -> 39.8 us  [exchange(): return lax.all_to_all(chunks, axes, 0, 0, axis_index_groups=[order])]
where the time goes in v4:
time: 60 us; the launch traced here: 59.8 us
  blocking collectives  39.8 us (66%)
  Pallas kernels  14.7 us (24%)
  starting transfers between devices  2.58 us (4%)
  waiting for transfers between devices  2.03 us (3%)
  between operations  0.69 us (1%)
    all_to_all x3, blocking collectives, exchange(): return lax.all_to_all(chunks, axes, 0, 0, axis_index_groups=[order])  39.8 us
    pallas_call x1, Pallas kernels, transposed(): call(functools.partial(outer_kernel, cells), struct(mode_weight.shape), '...  3.69 us
    pallas_call x1, Pallas kernels, transposed(): call(functools.partial(grid_kernel, len(later)), (struct((channels, 2, SU...  3.53 us
    all_to_all x1, starting transfers between devices, exchange(): return lax.all_to_all(chunks, axes, 0, 0, axis_index_groups=[order])  2.58 us
    all_to_all x1, waiting for transfers between devices, exchange(): return lax.all_to_all(chunks, axes, 0, 0, axis_index_groups=[order])  2.03 us
    pallas_call x1, Pallas kernels, transposed(): call(functools.partial(result_kernel, scale), (struct(field_shape), struc...  1.94 us
    pallas_call x1, Pallas kernels, transposed(): call(functools.partial(local_kernel, scale), (struct(field_shape), struct...  1.89 us
    pallas_call x1, Pallas kernels, transposed(): call(functools.partial(back_kernel, cells, channels), struct((devices * S...  1.48 us
  transfers between devices with their start and end apart: 1, of which 1 were waited for; matrix products, arithmetic and copies ran while one was open for 0% of the time, Pallas kernels for 9%

profile of v4, /device:TPU:0, one launch (start us, length us, event | category | flops | bytes accessed | tf_op | source)
XLA Modules:
  0.0 59.8 jit_solution(14638384278825178684)
XLA Ops:
  0.6 3.5 %grid.1 = (f32[32,2,8,128]{3,2,1,0:T(8,128)S(1)}, bf16[8,256,128]{2,1,0:T(8,128)(2,1)S(1)}, bf16[8,256,128]{2,1,0:T(8,128)(2,1)S(1)}, bf16[256,128]{1,0:T(8,128)...) custom-call(bf16[32,8,8,128]{3,2,1,0:T(8,128)(2,1)} %bitcast.28, ...), custom_call_target="tpu_custom_call" | custom-call | tf_op jit(solution)/shard_map/grid/pallas_call | solution.py:729
  4.2 16.5 %all_to_all.20.r_ref = f32[32,2,8,128]{3,2,1,0:T(8,128)S(1)} all-to-all(f32[32,2,8,128]{3,2,1,0:T(8,128)S(1)} %get-tuple-element.22), channel_id=1, replica_groups={{4,5,2,3,0,1,6,7,12,13,10,11,8,9,14,15,20,21,18,19,16,17,22,23,28,29,26..., dimensions={0} | all-to-all | bytes 524288 | tf_op jit(solution)/shard_map/all_to_all | solution.py:719
  20.6 0.0 copy-start.1
  20.6 0.7 %plane.1 = (f32[32,16,128]{2,1,0:T(8,128)S(1)}, f32[2,8,128]{2,1,0:T(8,128)S(1)}) custom-call(f32[32,2,8,128]{3,2,1,0:T(8,128)S(1)} %all_to_all.20.r_ref, bf16[512,512]{1,0:T(8,128)(2,1)S(1)} %get-tuple-element.23.txh_ref, bf16[512,512]{1,0:T(8,128)(2,1)S(1)} %get-tuple-element.24.txl_ref, bf16[128,256]{1,0:T(8,128)(2,1)S(1)} %get-tuple-element.25.tyh_ref, ...), custom_call_target="tpu_custom_call" | custom-call | tf_op jit(solution)/shard_map/plane/pallas_call | solution.py:760
  21.4 0.0 copy-start
  21.4 12.5 %all_to_all.21 = f32[32,16,128]{2,1,0:T(8,128)S(1)} all-to-all(f32[32,16,128]{2,1,0:T(8,128)S(1)} %get-tuple-element.27), channel_id=1, replica_groups={{4,5,2,3,0,1,6,7,12,13,10,11,8,9,14,15,20,21,18,19,16,17,22,23,28,29,26..., dimensions={0} | all-to-all | bytes 524288 | tf_op jit(solution)/shard_map/all_to_all | solution.py:719
  33.9 1.5 %back.1 = f32[256,128]{1,0:T(8,128)S(1)} custom-call(f32[512,128]{1,0:T(8,128)S(1)} %bitcast.24, f32[8,4,2,16,1024]{4,3,2,1,0:T(8,128)S(1)} %get-tuple-element.28.weight_ref), custom_call_target="tpu_custom_call" | custom-call | tf_op jit(solution)/shard_map/back/pallas_call | solution.py:779
  35.4 10.8 %all_to_all.22.r_ref = f32[32,8,128]{2,1,0:T(8,128)S(1)} all-to-all(f32[32,8,128]{2,1,0:T(8,128)S(1)} %bitcast.27), channel_id=1, replica_groups={{4,5,2,3,0,1,6,7,12,13,10,11,8,9,14,15,20,21,18,19,16,17,22,23,28,29,26..., dimensions={0} | all-to-all | bytes 262144 | tf_op jit(solution)/shard_map/all_to_all | solution.py:719
  46.2 1.4 %inverse.1 = f32[32,8,128]{2,1,0:T(8,128)} custom-call(f32[32,8,128]{2,1,0:T(8,128)S(1)} %all_to_all.22.r_ref, f32[2,8,128]{2,1,0:T(8,128)S(1)} %get-tuple-element.29.stat_ref, bf16[64,128]{1,0:T(8,128)(2,1)S(1)} %get-tuple-element.30.tyh_ref, bf16[64,128]{1,0:T(8,128)(2,1)S(1)} %get-tuple-element.31.tyl_ref, ...), custom_call_target="tpu_custom_call" | custom-call | tf_op jit(solution)/shard_map/inverse/pallas_call | solution.py:796
  47.6 2.6 %all-to-all-start.3 = ((f32[32,8,128]{2,1,0:T(8,128)}), f32[32,8,128]{2,1,0:T(8,128)S(1)}, u32[]{:S(2)}, u32[]{:S(2)}) async-start(f32[32,8,128]{2,1,0:T(8,128)} %inverse.1), calls=%async_computation.3 | async-start | bytes 262144 | tf_op jit(solution)/shard_map/all_to_all | solution.py:719
  50.2 0.0 copy-done.1
  50.2 1.9 %local.1 = (f32[32,8,8,128]{3,2,1,0:T(8,128)S(1)}, f32[1,32]{1,0:T(1,128)}) custom-call(f32[32,32]{1,0:T(8,128)S(1)} %copy-done.1, bf16[8,256,128]{2,1,0:T(8,128)(2,1)S(1)} %get-tuple-element.34.ghi_ref, bf16[8,256,128]{2,1,0:T(8,128)(2,1)S(1)} %get-tuple-element.35.glo_ref, f32[2,8,128]{2,1,0:T(8,128)S(1)} %get-tuple-element.29.stat_ref), custom_call_target="tpu_custom_call" | custom-call | tf_op jit(solution)/shard_map/local/pallas_call | solution.py:770
  52.1 0.0 copy-done
  52.1 3.7 %outer.1 = f32[8,4,2,16,1024]{4,3,2,1,0:T(8,128)} custom-call(f32[512,128]{1,0:T(8,128)S(1)} %bitcast.25, bf16[128,1152]{1,0:T(8,128)(2,1)S(1)} %copy-done), custom_call_target="tpu_custom_call" | custom-call | tf_op jit(solution)/shard_map/outer/pallas_call | solution.py:788
  55.8 2.0 %all-to-all-done.3 = f32[32,8,128]{2,1,0:T(8,128)S(1)} async-done(((f32[32,8,128]{2,1,0:T(8,128)}), f32[32,8,128]{2,1,0:T(8,128)S(1)}, u32[]{:S(2)}, u32[]{:S(2)}) %all-to-all-start.3) | async-done | bytes 131104 | tf_op jit(solution)/shard_map/all_to_all | solution.py:719
  57.9 1.9 %result.1 = (f32[32,8,8,128]{3,2,1,0:T(8,128)}, f32[32,32]{1,0:T(8,128)}) custom-call(f32[256,128]{1,0:T(8,128)S(1)} %bitcast.26, bf16[256,128]{1,0:T(8,128)(2,1)S(1)} %get-tuple-element.32.hi_ref, bf16[256,128]{1,0:T(8,128)(2,1)S(1)} %get-tuple-element.33.lo_ref, f32[32,8,8,128]{3,2,1,0:T(8,128)S(1)} %get-tuple-element.36.local_ref), custom_call_target="tpu_custom_call" | custom-call | tf_op jit(solution)/shard_map/result/pallas_call | solution.py:804
Async XLA Ops:
  20.6 29.6 %copy-start.1 = (f32[32,32]{1,0:T(8,128)S(1)}, f32[32,32]{1,0:T(8,128)}, u32[]{:S(2)}) copy-start(f32[32,32]{1,0:T(8,128)} %weight_ref.1) | copy-start | bytes 12292
  21.4 30.8 %copy-start = (bf16[128,1152]{1,0:T(8,128)(2,1)S(1)}, bf16[128,1152]{1,0:T(8,128)(2,1)}, u32[]{:S(2)}) copy-start(bf16[128,1152]{1,0:T(8,128)(2,1)} %constant.26.clone.spread_ref) | copy-start | bytes 884740
  47.6 10.2 %all-to-all-start.3 = ((f32[32,8,128]{2,1,0:T(8,128)}), f32[32,8,128]{2,1,0:T(8,128)S(1)}, u32[]{:S(2)}, u32[]{:S(2)}) async-start(f32[32,8,128]{2,1,0:T(8,128)} %inverse.1), calls=%async_computation.3 | async-start | bytes 262144 | tf_op jit(solution)/shard_map/all_to_all | solution.py:719

commit v5 on v4

--- a/solution.py
+++ b/solution.py
@@ -662,10 +662,12 @@
         block = dot(jnp.concatenate([left, left], axis=1), jnp.concatenate(right, axis=0))
         for k in range(places):
             part = block[:, k * LANES : (k + 1) * LANES]
-            grad_ref[:, first + k] = part.reshape(tile) + local_ref[:, first + k]
-        at = (slice(None), pl.ds(first, places))
-        copies.append(pltpu.make_async_copy(grad_ref.at[at], grad_hbm.at[at], sems.at[index]))
-        copies[-1].start()
+            x = first + k
+            grad_ref[:, x] = part.reshape(tile) + local_ref[:, x]
+            copies.append(
+                pltpu.make_async_copy(grad_ref.at[:, x], grad_hbm.at[:, x], sems.at[x])
+            )
+            copies[-1].start()
     point = jnp.zeros(point_ref.shape, F32)
     for y in range(y_local):
         taken = r_ref[pl.ds(y, channels, stride=SUBLANES), :]

time: 60 us -> 60.1 us (level)
  no operation moved by 1% of the time
where the time goes in v5:
time: 60.1 us; the launch traced here: 59.8 us
  blocking collectives  39.8 us (66%)
  Pallas kernels  14.7 us (24%)
  starting transfers between devices  2.58 us (4%)
  waiting for transfers between devices  2.03 us (3%)
  between operations  0.69 us (1%)
    all_to_all x3, blocking collectives, exchange(): return lax.all_to_all(chunks, axes, 0, 0, axis_index_groups=[order])  39.8 us
    pallas_call x1, Pallas kernels, transposed(): call(functools.partial(outer_kernel, cells), struct(mode_weight.shape), '...  3.69 us
    pallas_call x1, Pallas kernels, transposed(): call(functools.partial(grid_kernel, len(later)), (struct((channels, 2, SU...  3.53 us
    all_to_all x1, starting transfers between devices, exchange(): return lax.all_to_all(chunks, axes, 0, 0, axis_index_groups=[order])  2.58 us
    all_to_all x1, waiting for transfers between devices, exchange(): return lax.all_to_all(chunks, axes, 0, 0, axis_index_groups=[order])  2.03 us
    pallas_call x1, Pallas kernels, transposed(): call(functools.partial(result_kernel, scale), (struct(field_shape), struc...  1.95 us
    pallas_call x1, Pallas kernels, transposed(): call(functools.partial(local_kernel, scale), (struct(field_shape), struct...  1.89 us
    pallas_call x1, Pallas kernels, transposed(): call(functools.partial(back_kernel, cells, channels), struct((devices * S...  1.48 us
  transfers between devices with their start and end apart: 1, of which 1 were waited for; matrix products, arithmetic and copies ran while one was open for 0% of the time, Pallas kernels for 9%

profile of v5, /device:TPU:0, one launch (start us, length us, event | category | flops | bytes accessed | tf_op | source)
XLA Modules:
  0.0 59.8 jit_solution(13217955735926295561)
XLA Ops:
  0.6 3.5 %grid.1 = (f32[32,2,8,128]{3,2,1,0:T(8,128)S(1)}, bf16[8,256,128]{2,1,0:T(8,128)(2,1)S(1)}, bf16[8,256,128]{2,1,0:T(8,128)(2,1)S(1)}, bf16[256,128]{1,0:T(8,128)...) custom-call(bf16[32,8,8,128]{3,2,1,0:T(8,128)(2,1)} %bitcast.28, ...), custom_call_target="tpu_custom_call" | custom-call | tf_op jit(solution)/shard_map/grid/pallas_call | solution.py:731
  4.2 16.5 %all_to_all.20.r_ref = f32[32,2,8,128]{3,2,1,0:T(8,128)S(1)} all-to-all(f32[32,2,8,128]{3,2,1,0:T(8,128)S(1)} %get-tuple-element.22), channel_id=1, replica_groups={{4,5,2,3,0,1,6,7,12,13,10,11,8,9,14,15,20,21,18,19,16,17,22,23,28,29,26..., dimensions={0} | all-to-all | bytes 524288 | tf_op jit(solution)/shard_map/all_to_all | solution.py:721
  20.6 0.0 copy-start.1
  20.6 0.7 %plane.1 = (f32[32,16,128]{2,1,0:T(8,128)S(1)}, f32[2,8,128]{2,1,0:T(8,128)S(1)}) custom-call(f32[32,2,8,128]{3,2,1,0:T(8,128)S(1)} %all_to_all.20.r_ref, bf16[512,512]{1,0:T(8,128)(2,1)S(1)} %get-tuple-element.23.txh_ref, bf16[512,512]{1,0:T(8,128)(2,1)S(1)} %get-tuple-element.24.txl_ref, bf16[128,256]{1,0:T(8,128)(2,1)S(1)} %get-tuple-element.25.tyh_ref, ...), custom_call_target="tpu_custom_call" | custom-call | tf_op jit(solution)/shard_map/plane/pallas_call | solution.py:762
  21.4 0.0 copy-start
  21.4 12.5 %all_to_all.21 = f32[32,16,128]{2,1,0:T(8,128)S(1)} all-to-all(f32[32,16,128]{2,1,0:T(8,128)S(1)} %get-tuple-element.27), channel_id=1, replica_groups={{4,5,2,3,0,1,6,7,12,13,10,11,8,9,14,15,20,21,18,19,16,17,22,23,28,29,26..., dimensions={0} | all-to-all | bytes 524288 | tf_op jit(solution)/shard_map/all_to_all | solution.py:721
  33.9 1.5 %back.1 = f32[256,128]{1,0:T(8,128)S(1)} custom-call(f32[512,128]{1,0:T(8,128)S(1)} %bitcast.24, f32[8,4,2,16,1024]{4,3,2,1,0:T(8,128)S(1)} %get-tuple-element.28.weight_ref), custom_call_target="tpu_custom_call" | custom-call | tf_op jit(solution)/shard_map/back/pallas_call | solution.py:781
  35.4 10.8 %all_to_all.22.r_ref = f32[32,8,128]{2,1,0:T(8,128)S(1)} all-to-all(f32[32,8,128]{2,1,0:T(8,128)S(1)} %bitcast.27), channel_id=1, replica_groups={{4,5,2,3,0,1,6,7,12,13,10,11,8,9,14,15,20,21,18,19,16,17,22,23,28,29,26..., dimensions={0} | all-to-all | bytes 262144 | tf_op jit(solution)/shard_map/all_to_all | solution.py:721
  46.2 1.4 %inverse.1 = f32[32,8,128]{2,1,0:T(8,128)} custom-call(f32[32,8,128]{2,1,0:T(8,128)S(1)} %all_to_all.22.r_ref, f32[2,8,128]{2,1,0:T(8,128)S(1)} %get-tuple-element.29.stat_ref, bf16[64,128]{1,0:T(8,128)(2,1)S(1)} %get-tuple-element.30.tyh_ref, bf16[64,128]{1,0:T(8,128)(2,1)S(1)} %get-tuple-element.31.tyl_ref, ...), custom_call_target="tpu_custom_call" | custom-call | tf_op jit(solution)/shard_map/inverse/pallas_call | solution.py:798
  47.6 2.6 %all-to-all-start.3 = ((f32[32,8,128]{2,1,0:T(8,128)}), f32[32,8,128]{2,1,0:T(8,128)S(1)}, u32[]{:S(2)}, u32[]{:S(2)}) async-start(f32[32,8,128]{2,1,0:T(8,128)} %inverse.1), calls=%async_computation.3 | async-start | bytes 262144 | tf_op jit(solution)/shard_map/all_to_all | solution.py:721
  50.2 0.0 copy-done.1
  50.2 1.9 %local.1 = (f32[32,8,8,128]{3,2,1,0:T(8,128)S(1)}, f32[1,32]{1,0:T(1,128)}) custom-call(f32[32,32]{1,0:T(8,128)S(1)} %copy-done.1, bf16[8,256,128]{2,1,0:T(8,128)(2,1)S(1)} %get-tuple-element.34.ghi_ref, bf16[8,256,128]{2,1,0:T(8,128)(2,1)S(1)} %get-tuple-element.35.glo_ref, f32[2,8,128]{2,1,0:T(8,128)S(1)} %get-tuple-element.29.stat_ref), custom_call_target="tpu_custom_call" | custom-call | tf_op jit(solution)/shard_map/local/pallas_call | solution.py:772
  52.1 0.0 copy-done
  52.1 3.7 %outer.1 = f32[8,4,2,16,1024]{4,3,2,1,0:T(8,128)} custom-call(f32[512,128]{1,0:T(8,128)S(1)} %bitcast.25, bf16[128,1152]{1,0:T(8,128)(2,1)S(1)} %copy-done), custom_call_target="tpu_custom_call" | custom-call | tf_op jit(solution)/shard_map/outer/pallas_call | solution.py:790
  55.8 2.0 %all-to-all-done.3 = f32[32,8,128]{2,1,0:T(8,128)S(1)} async-done(((f32[32,8,128]{2,1,0:T(8,128)}), f32[32,8,128]{2,1,0:T(8,128)S(1)}, u32[]{:S(2)}, u32[]{:S(2)}) %all-to-all-start.3) | async-done | bytes 131104 | tf_op jit(solution)/shard_map/all_to_all | solution.py:721
  57.9 1.9 %result.1 = (f32[32,8,8,128]{3,2,1,0:T(8,128)}, f32[32,32]{1,0:T(8,128)}) custom-call(f32[256,128]{1,0:T(8,128)S(1)} %bitcast.26, bf16[256,128]{1,0:T(8,128)(2,1)S(1)} %get-tuple-element.32.hi_ref, bf16[256,128]{1,0:T(8,128)(2,1)S(1)} %get-tuple-element.33.lo_ref, f32[32,8,8,128]{3,2,1,0:T(8,128)S(1)} %get-tuple-element.36.local_ref), custom_call_target="tpu_custom_call" | custom-call | tf_op jit(solution)/shard_map/result/pallas_call | solution.py:806
Async XLA Ops:
  20.6 29.6 %copy-start.1 = (f32[32,32]{1,0:T(8,128)S(1)}, f32[32,32]{1,0:T(8,128)}, u32[]{:S(2)}) copy-start(f32[32,32]{1,0:T(8,128)} %weight_ref.1) | copy-start | bytes 12292
  21.4 30.8 %copy-start = (bf16[128,1152]{1,0:T(8,128)(2,1)S(1)}, bf16[128,1152]{1,0:T(8,128)(2,1)}, u32[]{:S(2)}) copy-start(bf16[128,1152]{1,0:T(8,128)(2,1)} %constant.26.clone.spread_ref) | copy-start | bytes 884740
  47.6 10.2 %all-to-all-start.3 = ((f32[32,8,128]{2,1,0:T(8,128)}), f32[32,8,128]{2,1,0:T(8,128)S(1)}, u32[]{:S(2)}, u32[]{:S(2)}) async-start(f32[32,8,128]{2,1,0:T(8,128)} %inverse.1), calls=%async_computation.3 | async-start | bytes 262144 | tf_op jit(solution)/shard_map/all_to_all | solution.py:721
